TPU v7x, 32 devices: a whole 2x2x4 slice. The times are simulated.
32 devices in a mesh: group: 2 (over core), trow: 2 (over y), tcol: 8 (over z, x).
Axes of the slice: x: 2, y: 2, z: 4, core: 2. Of those that a mesh axis runs over, the one named last changes fastest.
Arguments:
- displacement: float32 [3, 128, 64, 256], P(None, ('group', 'trow'), 'tcol'), may hold values from -6 to 6
- velocity: float32 [3, 128, 64, 256], P(None, ('group', 'trow'), 'tcol'), may hold values from -6 to 6
- stiffness: float32 [128, 64], P(('group', 'trow'), 'tcol'), may hold values from 4 to 12
- wet_position: float32 [3, 8192], P(None, ('group', 'trow', 'tcol')), may hold values from -6 to 6
- wet_normal: float32 [3, 8192], P(None, ('group', 'trow', 'tcol')), may hold values from -6 to 6
- wet_area: float32 [8192], P(('group', 'trow', 'tcol')), may hold values from 0.022097087 to 0.22097087
- wet_map: int32 [8192], P(('group', 'trow', 'tcol')), may hold values from 0 to 255
Outputs:
- displacement_out: float32 [3, 128, 64, 256], P(None, ('group', 'trow'), 'tcol')
- velocity_out: float32 [3, 128, 64, 256], P(None, ('group', 'trow'), 'tcol')
Inputs may be any that keep to these rules, and one draw needn't show every extreme that they name: Each wet point lies on the patch of nodes of the device that holds it: wet_map gives a * 8 + b for the node (a, b) of that patch.
All inputs are finite; a program needn't handle non-finite values.
Results may differ from a plain program's by a relative error of at most 0.0018.
Values may be sent and summed in bfloat16 or wider, within the bound.
A program may use at most 128 MiB of HBM per device.

v0:
```python
import functools
import math

import jax
import jax.numpy as jnp
from jax import lax
from jax.experimental import pallas as pl
from jax.experimental.pallas import tpu as pltpu
from jax.sharding import PartitionSpec as P

LOADS = 64
SUBSTEPS = 4
COUPLED = 2

SPHERE_AREA = 4.0 * math.pi
SMOOTHING = 0.1
TIME_STEP = 0.3
THICKNESS = 0.5
SPLINE_TAPS = (2.0 / 3.0, -1.0 / 12.0, -1.0 / 12.0, -1.0 / 6.0)
REACH = 3
PAD = 8
MESH = pl.DeviceIdType.MESH
VMEM = pltpu.VMEM


def row_device(index, trow_count):
    return {"group": index // trow_count, "trow": lax.rem(index, trow_count)}


def whole_spec():
    return pl.BlockSpec(memory_space=pltpu.VMEM)


HIGHEST = lax.Precision.HIGHEST


def coupled_kernel(
    shape, u_in, v_in, stiff_ref, position_ref, normal_ref, area_ref, node_ref, u_out, v_out,
    field, speed_now, work, load, col_out, col_in, row_out, row_in,
    geometry, sources, targets, target_cols, normal_cols, pick, spread,
    own_speeds, packed_out, packed_in, unpacked, tiles, partial_out, partial_in,
    halo_send, halo_recv, geo_send, geo_recv, speed_send, speed_recv, part_send, part_recv
):
    col_count, row_count, trow_count = shape
    parts, breadth, height, width = speed_now.shape
    half = width // 2
    points = geometry.shape[1]
    count = breadth * height
    col = lax.axis_index("tcol")
    row = lax.axis_index("group") * trow_count + lax.axis_index("trow")
    present = (col > 0, col < col_count - 1, row > 0, row < row_count - 1)
    peers = (
        {"tcol": jnp.maximum(col - 1, 0)},
        {"tcol": jnp.minimum(col + 1, col_count - 1)},
        row_device(jnp.maximum(row - 1, 0), trow_count),
        row_device(jnp.minimum(row + 1, row_count - 1), trow_count),
    )
    middle = pl.ds(PAD, height)

    def col_peer(d):
        return {"tcol": lax.rem(col + d, col_count)}

    def row_peer(d):
        return row_device(lax.rem(row + d, row_count), trow_count)

    barrier = pltpu.get_barrier_semaphore()

    @pl.loop(1, col_count)
    def _(d):
        pl.semaphore_signal(barrier, inc=1, device_id=col_peer(d), device_id_type=MESH)

    @pl.loop(1, row_count)
    def _(d):
        pl.semaphore_signal(barrier, inc=1, device_id=row_peer(d), device_id_type=MESH)

    geometry[0:3, :] = position_ref[...]
    geometry[3:6, :] = normal_ref[...] * (area_ref[...] * (1.0 / SPHERE_AREA))
    geometry[6:8, :] = jnp.zeros((2, points), jnp.float32)
    pl.semaphore_wait(barrier, col_count + row_count - 2)

    def geo_copy(kind, d):
        return pltpu.make_async_remote_copy(
            src_ref=geometry,
            dst_ref=sources.at[col] if kind == 0 else targets.at[row],
            send_sem=geo_send.at[kind, d],
            recv_sem=geo_recv.at[kind, d],
            device_id=col_peer(d) if kind == 0 else row_peer(d),
            device_id_type=MESH,
        )

    def speed_copy(repeat, d):
        return pltpu.make_async_remote_copy(
            src_ref=packed_out.at[repeat],
            dst_ref=packed_in.at[repeat, col],
            send_sem=speed_send.at[repeat, d],
            recv_sem=speed_recv.at[repeat, d],
            device_id=col_peer(d),
            device_id_type=MESH,
        )

    def part_copy(repeat, d):
        return pltpu.make_async_remote_copy(
            src_ref=partial_out.at[repeat, lax.rem(row + d, row_count)],
            dst_ref=partial_in.at[repeat, d],
            send_sem=part_send.at[repeat, d],
            recv_sem=part_recv.at[repeat, d],
            device_id=row_peer(d),
            device_id_type=MESH,
        )

    for kind, total in ((1, row_count), (0, col_count)):

        @pl.loop(1, total)
        def _(d):
            geo_copy(kind, d).start()

    sources[col] = geometry[...]
    targets[row] = geometry[...]

    field[...] = jnp.zeros_like(field)
    for part in range(parts):
        for j in range(breadth):
            for lanes in range(2):
                lines = pl.ds(lanes * breadth + j, height, stride=2 * breadth)
                cut = pl.ds(lanes * half, half)
                field[part, REACH + j, middle, cut] = u_in[part, lines, :]
                speed_now[part, j, :, cut] = v_in[part, lines, :]
    for side in range(2):

        @pl.when(jnp.logical_not(present[side]))
        def _():
            col_in[:, :, side] = jnp.zeros(col_in.shape[:2] + col_in.shape[3:], col_in.dtype)

    def as_column(line):
        return jnp.broadcast_to(line, (half, line.shape[1])).T

    for part in range(parts):
        normal_cols[part] = as_column(normal_ref[part : part + 1, :])
    spread[...] = (
        lax.broadcasted_iota(jnp.int32, (count, points), 0) == node_ref[...]
    ).astype(jnp.float32)
    pick[...] = spread[...].T

    def halo_copy(step, side, part, arriving):
        out_buffer, in_buffer = (col_out, col_in) if side < 2 else (row_out, row_in)
        own = side % 2
        other = own if arriving else 1 - own
        return pltpu.make_async_remote_copy(
            src_ref=out_buffer.at[step, part, own],
            dst_ref=in_buffer.at[step, part, other],
            send_sem=halo_send.at[step, part, side],
            recv_sem=halo_recv.at[step, part, (side // 2) * 2 + other],
            device_id=peers[side],
            device_id_type=MESH,
        )

    lane = lax.broadcasted_iota(jnp.int32, (height, half), 1)
    low = lane < half // 2
    low_half = lax.broadcasted_iota(jnp.int32, (points // 2, half), 1) < half // 2

    def pack(value):
        turned = pltpu.roll(value[points // 2 :], half // 2, 1)
        return jnp.where(low_half, turned, value[: points // 2])

    def tile(r):
        group = 32

        def block(index, carry):
            source = index // (points // half)
            lanes = pl.ds(pl.multiple_of(lax.rem(index, points // half) * half, half), half)
            line = [sources[source, k : k + 1, lanes] for k in range(6)]

            def rows_of(g, inner):
                rows = pl.ds(pl.multiple_of(g * group, group), group)
                dx = target_cols[r, 0, rows, :] - line[0]
                dy = target_cols[r, 1, rows, :] - line[1]
                dz = target_cols[r, 2, rows, :] - line[2]
                numerator = line[3] * dx + line[4] * dy + line[5] * dz
                squared = dx * dx + dy * dy + dz * dz + SMOOTHING * SMOOTHING
                inverse = lax.rsqrt(squared)
                value = numerator * inverse * (inverse * inverse)
                tiles[r, source, rows, lanes] = value.astype(jnp.bfloat16)
                return inner

            return lax.fori_loop(0, points // group, rows_of, carry, unroll=2)

        lax.fori_loop(0, col_count * (points // half), block, 0)

    def send_halos(step, part):
        for side, first in ((0, REACH), (1, breadth)):

            @pl.when(present[side])
            def _():
                for j in range(REACH):
                    col_out[step, part, side, j] = field[part, first + j, middle, :].astype(
                        col_out.dtype
                    )
                halo_copy(step, side, part, False).start()

        for side, first in ((2, PAD), (3, PAD + height - REACH)):

            @pl.when(present[side])
            def _():
                for j in range(breadth):
                    row_out[
                        step, part, side - 2, j // 2, (j % 2) * 4 : (j % 2) * 4 + REACH, :
                    ] = field[part, REACH + j, first : first + REACH, :]
                halo_copy(step, side, part, False).start()

    def local(part):
        def body(column, carry):
            a = field[part, REACH + column, middle, 0:half]
            b = field[part, REACH + column, middle, half:width]
            turned_a = pltpu.roll(a, half // 2, 1)
            turned_b = pltpu.roll(b, half // 2, 1)
            between = jnp.where(low, turned_a, turned_b)
            edge_a = jnp.where(low, a, turned_a)
            edge_b = jnp.where(low, turned_b, b)
            stiff = stiff_ref[column]
            for lanes, here, edge in ((0, a, edge_a), (1, b, edge_b)):
                cut = pl.ds(lanes * half, half)
                summed = (2.0 * SPLINE_TAPS[0]) * here
                for offset in range(1, REACH + 1):
                    summed = summed + SPLINE_TAPS[offset] * (
                        field[part, REACH + column + offset, middle, cut]
                        + field[part, REACH + column - offset, middle, cut]
                    )
                value = -(stiff * summed) - THICKNESS * (2.0 * here - between - edge)
                if lanes == 1:
                    value = value + load[part, column]
                work[part, column, :, cut] = speed_now[part, column, :, cut] + TIME_STEP * value
            return carry

        lax.fori_loop(0, breadth, body, 0)

    def complete(step, part):
        for side, first in ((2, PAD - REACH), (3, PAD + height)):

            @pl.when(present[side])
            def _():
                halo_copy(step, side, part, True).wait_recv()
                for j in range(breadth):
                    field[part, REACH + j, first : first + REACH, :] = row_in[
                        step, part, side - 2, j // 2, (j % 2) * 4 : (j % 2) * 4 + REACH, :
                    ]

        def along_rows(column, carry):
            stiff = stiff_ref[column] * (-TIME_STEP)
            for lanes in range(2):
                cut = pl.ds(lanes * half, half)
                summed = 0.0
                for offset in range(1, REACH + 1):
                    summed = summed + SPLINE_TAPS[offset] * (
                        field[part, REACH + column, pl.ds(PAD + offset, height), cut]
                        + field[part, REACH + column, pl.ds(PAD - offset, height), cut]
                    )
                work[part, column, :, cut] += stiff * summed
            return carry

        lax.fori_loop(0, breadth, along_rows, 0)

        for side in range(2):

            @pl.when(present[side])
            def _():
                halo_copy(step, side, part, True).wait_recv()

        for column in range(breadth):
            stiff = stiff_ref[column] * (-TIME_STEP)
            for lanes in range(2):
                cut = pl.ds(lanes * half, half)
                value = work[part, column, :, cut]
                summed = None
                for offset in range(1, REACH + 1):
                    for side, j in ((0, column - offset + REACH), (1, column + offset - breadth)):
                        inside = (column - offset < 0) if side == 0 else (column + offset >= breadth)
                        if inside:
                            term = SPLINE_TAPS[offset] * col_in[
                                step, part, side, j, :, cut
                            ].astype(jnp.float32)
                            summed = term if summed is None else summed + term
                if summed is not None:
                    value = value + stiff * summed
                speed_now[part, column, :, cut] = value
                field[part, REACH + column, middle, cut] += TIME_STEP * value

    for repeat in range(COUPLED):
        speeds = jnp.zeros((points, half), jnp.float32)
        for part in range(parts):
            outer = speed_now[part, :, :, half:width].reshape(count, half)
            picked = jnp.dot(
                pick[...], outer, precision=HIGHEST, preferred_element_type=jnp.float32
            )
            speeds = speeds + normal_cols[part] * picked
        own_speeds[...] = speeds
        packed_out[repeat] = pack(speeds).astype(packed_out.dtype)

        @pl.loop(1, col_count)
        def _(d):
            speed_copy(repeat, d).start()

        packed_in[repeat, col] = packed_out[repeat]

        if repeat == 0:

            @pl.loop(1, row_count)
            def _(d):
                geo_copy(1, d).wait_recv()

            @pl.loop(1, col_count)
            def _(d):
                geo_copy(0, d).wait_recv()

            @pl.loop(0, row_count)
            def _(r):
                for k in range(3):
                    target_cols[r, k] = as_column(targets[r, k : k + 1, :])

            tile(lax.rem(row + 1, row_count))

        @pl.loop(1, col_count)
        def _(d):
            speed_copy(repeat, d).wait_recv()

        @pl.loop(0, parts)
        def _(part):
            send_halos(repeat * SUBSTEPS, part)

        @pl.loop(0, col_count)
        def _(c):
            value = packed_in[repeat, c].astype(jnp.float32)
            unpacked[c, 0 : points // 2, :] = value.astype(jnp.bfloat16)
            unpacked[c, points // 2 : points, :] = pltpu.roll(value, half // 2, 1).astype(
                jnp.bfloat16
            )

        @pl.loop(1, row_count + 1)
        def _(d):
            r = lax.rem(row + d, row_count)
            total = jnp.zeros((points, half), jnp.float32)
            for c in range(col_count):
                total = total + jnp.dot(
                    tiles[r, c], unpacked[c], preferred_element_type=jnp.float32
                )
            partial_out[repeat, r] = pack(total)

            @pl.when(d < row_count)
            def _():
                part_copy(repeat, d).start()
                if repeat == 0:
                    tile(lax.rem(r + 1, row_count))

        received = partial_out[repeat, row]
        for d in range(1, row_count):
            part_copy(repeat, d).wait_recv()
            received = received + partial_in[repeat, d]
        low_points = jnp.concatenate([low_half, low_half], axis=0)
        both = jnp.concatenate([received, pltpu.roll(received, half // 2, 1)], axis=0)
        pressure = jnp.where(low_points, 0.0, 0.5 * own_speeds[...] + both)
        for part in range(parts):
            loading = jnp.dot(
                spread[...], -(normal_cols[part] * pressure),
                precision=HIGHEST, preferred_element_type=jnp.float32,
            )
            load[part] = loading.reshape(breadth, height, half)

            local(part)

        last = (repeat + 1) * SUBSTEPS - 1

        @pl.loop(repeat * SUBSTEPS, last + 1)
        def _(step):
            @pl.loop(0, parts)
            def _(part):
                complete(step, part)

                @pl.when(step < last)
                def _():
                    send_halos(step + 1, part)
                    local(part)

    for part in range(parts):
        for j in range(breadth):
            for lanes in range(2):
                lines = pl.ds(lanes * breadth + j, height, stride=2 * breadth)
                cut = pl.ds(lanes * half, half)
                u_out[part, lines, :] = field[part, REACH + j, middle, cut]
                v_out[part, lines, :] = speed_now[part, j, :, cut]

    @pl.loop(0, COUPLED * SUBSTEPS)
    def _(step):
        for side in range(4):

            @pl.when(present[side])
            def _():
                for part in range(parts):
                    halo_copy(step, side, part, False).wait_send()

    @pl.loop(1, col_count)
    def _(d):
        geo_copy(0, d).wait_send()
        for repeat in range(COUPLED):
            speed_copy(repeat, d).wait_send()

    @pl.loop(1, row_count)
    def _(d):
        geo_copy(1, d).wait_send()
        for repeat in range(COUPLED):
            part_copy(repeat, d).wait_send()


def on_device(shape, displacement, velocity, stiffness, wet_position, wet_normal, wet_area, wet_map):
    col_count, row_count, _ = shape
    parts, height, breadth, width = displacement.shape
    half = width // 2
    points = wet_map.shape[0]
    steps = COUPLED * SUBSTEPS
    stiff = jnp.broadcast_to(stiffness.T[:, :, None], (breadth, height, half))
    node = (wet_map % breadth) * height + wet_map // breadth

    def split(state):
        tiled = state.reshape(parts, height, breadth, 2, half).transpose(0, 1, 3, 2, 4)
        return tiled.reshape(parts, height * 2 * breadth, half)

    def joined(state):
        tiled = state.reshape(parts, height, 2, breadth, half).transpose(0, 1, 3, 2, 4)
        return tiled.reshape(parts, height, breadth, width)

    state = jax.ShapeDtypeStruct((parts, height * 2 * breadth, half), jnp.float32)
    cols = (steps, parts, 2, REACH, height, width)
    rows = (steps, parts, 2, breadth // 2, 8, width)
    f32, bf16 = jnp.float32, jnp.bfloat16
    dma = pltpu.SemaphoreType.DMA
    u_new, v_new = pl.pallas_call(
        functools.partial(coupled_kernel, shape),
        out_shape=(state, state),
        in_specs=[whole_spec()] * 7,
        out_specs=(whole_spec(), whole_spec()),
        scratch_shapes=[
            VMEM((parts, breadth + 2 * REACH, height + 2 * PAD, width), f32),
            VMEM((parts, breadth, height, width), f32),
            VMEM((parts, breadth, height, width), f32),
            VMEM((parts, breadth, height, half), f32),
            VMEM(cols, bf16),
            VMEM(cols, bf16),
            VMEM(rows, f32),
            VMEM(rows, f32),
            VMEM((8, points), f32),
            VMEM((col_count, 8, points), f32),
            VMEM((row_count, 8, points), f32),
            VMEM((row_count, 3, points, half), f32),
            VMEM((parts, points, half), f32),
            VMEM((points, height * breadth), f32),
            VMEM((height * breadth, points), f32),
            VMEM((points, half), f32),
            VMEM((COUPLED, points // 2, half), bf16),
            VMEM((COUPLED, col_count, points // 2, half), bf16),
            VMEM((col_count, points, half), bf16),
            VMEM((row_count, col_count, points, points), bf16),
            VMEM((COUPLED, row_count, points // 2, half), f32),
            VMEM((COUPLED, row_count, points // 2, half), f32),
            dma((steps, parts, 4)),
            dma((steps, parts, 4)),
            dma((2, max(col_count, row_count))),
            dma((2, max(col_count, row_count))),
            dma((COUPLED, col_count)),
            dma((COUPLED, col_count)),
            dma((COUPLED, row_count)),
            dma((COUPLED, row_count)),
        ],
        compiler_params=pltpu.CompilerParams(
            collective_id=0, has_side_effects=True, vmem_limit_bytes=67043328
        ),
        name="coupled_steps",
    )(
        split(displacement), split(velocity), stiff,
        wet_position, wet_normal, wet_area[None, :], node[None, :],
    )
    return (joined(u_new), joined(v_new))


def solution(mesh):
    sizes = mesh.shape
    shape = (sizes["tcol"], sizes["group"] * sizes["trow"], sizes["trow"])
    state = P(None, ("group", "trow"), "tcol", None)
    wet = ("group", "trow", "tcol")
    return jax.shard_map(
        functools.partial(on_device, shape),
        mesh=mesh,
        in_specs=(
            state,
            state,
            P(("group", "trow"), "tcol"),
            P(None, wet),
            P(None, wet),
            P(wet),
            P(wet),
        ),
        out_specs=(state, state),
        check_vma=False,
    )
```

profile of v0, /device:TPU:0, one launch (start us, length us, event | category | flops | bytes accessed | tf_op | source)
XLA Modules:
  0.0 99.8 jit_solution(12988091751508363114)
XLA Ops:
  0.6 0.0 copy-start.2
  0.6 0.0 copy-start.1
  0.6 0.7 copy-done.2
  1.3 0.6 fusion.1
  1.9 0.0 copy-done.1
  1.9 0.8 broadcast_in_dim.12.stiff_ref
  2.6 94.1 %coupled_steps.1 = (f32[3,512,128]{2,1,0:T(8,128)}, f32[3,512,128]{2,1,0:T(8,128)}) custom-call(f32[3,512,128]{2,1,0:T(8,128)} %bitcast.25, f32[3,512,128]{2,1,0:T(8,128)} %bitcast.26, f32[8,32,128]{2,1,0:T(8,128)} %broadcast_in_dim.12.stiff_ref, f32[3,256]{1,0:T(4,128)} %position_ref.1, f32[3,256]{1,0:T(4,128)} %normal_ref.1, f32[1,256]{1,0:T(1,128)} %bitcast.29, ...), custom_call_target="tpu_custom_call" | custom-call | tf_op jit(solution)/shard_map/coupled_steps/pallas_call | solution.py:434
  96.7 0.0 copy-start
  96.7 2.1 %copy.11 = f32[3,32,8,256]{3,2,1,0:T(8,128)} copy(f32[3,32,8,256]{3,2,1,0:T(8,128)} %bitcast.24) | data formatting | bytes 1572864
  98.9 0.0 copy-done
  98.9 0.9 copy.12
Async XLA Ops:
  0.6 0.7 copy-start.2
  0.6 1.2 %copy-start.1 = (f32[32,8]{0,1:T(8,128)S(1)}, f32[32,8]{0,1:T(8,128)}, u32[]{:S(2)}) copy-start(f32[32,8]{0,1:T(8,128)} %param.9) | copy-start | bytes 3076
  96.7 2.1 %copy-start = (f32[3,512,128]{2,1,0:T(8,128)S(1)}, f32[3,512,128]{2,1,0:T(8,128)}, u32[]{:S(2)}) copy-start(f32[3,512,128]{2,1,0:T(8,128)} %get-tuple-element.5) | copy-start | bytes 2359300
where the time goes:
time: 100 us; the launch traced here: 99.8 us
  Pallas kernels  94.1 us (94%)
  local copies, waits for them, and re-layouts  4.44 us (4%)
    pallas_call x1, Pallas kernels, on_device(): pl.pallas_call(functools.partial(coupled_kernel, shape), out_shape=(state...  94.1 us
    unnamed x8, local copies, waits for them, and re-layouts  3.69 us

commit v1 on v0

--- a/solution.py
+++ b/solution.py
@@ -39,7 +39,8 @@
     field, speed_now, work, load, col_out, col_in, row_out, row_in,
     geometry, sources, targets, target_cols, normal_cols, pick, spread,
     own_speeds, packed_out, packed_in, unpacked, tiles, partial_out, partial_in,
-    halo_send, halo_recv, geo_send, geo_recv, speed_send, speed_recv, part_send, part_recv
+    halo_send, halo_recv, geo_send, geo_recv, speed_send, speed_recv, part_send, part_recv,
+    all_out, all_in, all_send, all_recv
 ):
     col_count, row_count, trow_count = shape
     parts, breadth, height, width = speed_now.shape
@@ -76,7 +77,47 @@
     geometry[0:3, :] = position_ref[...]
     geometry[3:6, :] = normal_ref[...] * (area_ref[...] * (1.0 / SPHERE_AREA))
     geometry[6:8, :] = jnp.zeros((2, points), jnp.float32)
-    pl.semaphore_wait(barrier, col_count + row_count - 2)
+
+    total = col_count * row_count
+    me = row * col_count + col
+
+    def any_device(index):
+        r = index // col_count
+        return {"group": r // trow_count, "trow": lax.rem(r, trow_count), "tcol": lax.rem(index, col_count)}
+
+    @pl.loop(1, total)
+    def _(d):
+        pl.semaphore_signal(barrier, inc=1, device_id=any_device(lax.rem(me + d, total)), device_id_type=MESH)
+
+    pl.semaphore_wait(barrier, col_count + row_count - 2 + total - 1)
+
+    def all_copy(k, d):
+        to = lax.rem(me + d, total)
+        return pltpu.make_async_remote_copy(
+            src_ref=all_out.at[k, to], dst_ref=all_in.at[k, me],
+            send_sem=all_send.at[k, d], recv_sem=all_recv.at[k, d],
+            device_id=any_device(to), device_id_type=MESH)
+
+    def fill(k, carry):
+        def one(i, c):
+            all_out[k, i] = (all_in[lax.rem(k + 2, 3), i].astype(jnp.float32) + 1.0).astype(all_out.dtype) if False else jnp.zeros(all_out.shape[2:], all_out.dtype)
+            return c
+        lax.fori_loop(0, total, one, 0)
+
+        @pl.loop(1, total)
+        def _(d):
+            all_copy(k, d).start()
+
+        @pl.loop(1, total)
+        def _(d):
+            all_copy(k, d).wait_recv()
+
+        @pl.loop(1, total)
+        def _(d):
+            all_copy(k, d).wait_send()
+        return carry
+
+    lax.fori_loop(0, 1, fill, 0)
 
     def geo_copy(kind, d):
         return pltpu.make_async_remote_copy(
@@ -467,6 +508,10 @@
             dma((COUPLED, col_count)),
             dma((COUPLED, row_count)),
             dma((COUPLED, row_count)),
+            VMEM((1, col_count * row_count, 16, 128), jnp.int16),
+            VMEM((1, col_count * row_count, 16, 128), jnp.int16),
+            dma((1, col_count * row_count)),
+            dma((1, col_count * row_count)),
         ],
         compiler_params=pltpu.CompilerParams(
             collective_id=0, has_side_effects=True, vmem_limit_bytes=67043328

time: 100 us -> 106 us (1.060)
  Pallas kernels: 94.1 us -> 99.1 us
    pallas_call x1, Pallas kernels: 94.1 us -> 99.1 us  [on_device(): pl.pallas_call(functools.partial(coupled_kernel, shape), out_shape=(state...]
where the time goes in v1:
time: 106 us; the launch traced here: 105 us
  Pallas kernels  99.1 us (93%)
  local copies, waits for them, and re-layouts  4.44 us (4%)
    pallas_call x1, Pallas kernels, on_device(): pl.pallas_call(functools.partial(coupled_kernel, shape), out_shape=(state...  99.1 us
    unnamed x8, local copies, waits for them, and re-layouts  3.69 us

profile of v1, /device:TPU:0, one launch (start us, length us, event | category | flops | bytes accessed | tf_op | source)
XLA Modules:
  0.0 104.8 jit_solution(3876477277807205197)
XLA Ops:
  0.6 0.0 copy-start.2
  0.6 0.0 copy-start.1
  0.6 0.7 copy-done.2
  1.3 0.6 fusion.1
  1.9 0.0 copy-done.1
  1.9 0.8 broadcast_in_dim.12.stiff_ref
  2.6 99.1 %coupled_steps.1 = (f32[3,512,128]{2,1,0:T(8,128)}, f32[3,512,128]{2,1,0:T(8,128)}) custom-call(f32[3,512,128]{2,1,0:T(8,128)} %bitcast.25, f32[3,512,128]{2,1,0:T(8,128)} %bitcast.26, f32[8,32,128]{2,1,0:T(8,128)} %broadcast_in_dim.12.stiff_ref, f32[3,256]{1,0:T(4,128)} %position_ref.1, f32[3,256]{1,0:T(4,128)} %normal_ref.1, f32[1,256]{1,0:T(1,128)} %bitcast.29, ...), custom_call_target="tpu_custom_call" | custom-call | tf_op jit(solution)/shard_map/coupled_steps/pallas_call | solution.py:475
  101.8 0.0 copy-start
  101.8 2.1 %copy.11 = f32[3,32,8,256]{3,2,1,0:T(8,128)} copy(f32[3,32,8,256]{3,2,1,0:T(8,128)} %bitcast.24) | data formatting | bytes 1572864
  103.9 0.0 copy-done
  103.9 0.9 copy.12
Async XLA Ops:
  0.6 0.7 copy-start.2
  0.6 1.2 %copy-start.1 = (f32[32,8]{0,1:T(8,128)S(1)}, f32[32,8]{0,1:T(8,128)}, u32[]{:S(2)}) copy-start(f32[32,8]{0,1:T(8,128)} %param.9) | copy-start | bytes 3076
  101.8 2.1 %copy-start = (f32[3,512,128]{2,1,0:T(8,128)S(1)}, f32[3,512,128]{2,1,0:T(8,128)}, u32[]{:S(2)}) copy-start(f32[3,512,128]{2,1,0:T(8,128)} %get-tuple-element.5) | copy-start | bytes 2359300

commit v2 on v0

--- a/solution.py
+++ b/solution.py
@@ -479,13 +479,696 @@
     return (joined(u_new), joined(v_new))
 
 
+PAIR = 2
+LEVELS = 32767.0
+
+
+def plane_kernel(
+    shape, u_hbm, v_hbm, stiff_ref, position_ref, normal_ref, area_ref, map_ref, u_out, v_out,
+    u_raw, v_raw, perm, turn, eye, stencil, edges, in_out, in_in, facts_out, facts, places, targets,
+    source_cols, first_out, first_in, tiles, part_out, part_in, spoken,
+    onehot, onehot_back, u_now, v_now, load, halves, summed, beside, stiff_now, own_speed,
+    halo_out, halo_in, speed_out, speed_in, final_out, final_in, scale_out, scale_in,
+    load_sem, facts_send, facts_recv, places_send, places_recv, first_send, first_recv,
+    in_send, in_recv, part_send, part_recv, halo_send, halo_recv, speed_send, speed_recv,
+    final_send, final_recv, scale_send, scale_recv,
+):
+    col_count, row_count, trow_count = shape
+    depth_count = col_count // PAIR
+    members = row_count * PAIR
+    total = members * depth_count
+    parts, _, half = u_raw.shape
+    count, points = onehot.shape[1:]
+    breadth, height = stiff_ref.shape
+    width = perm.shape[1]
+    own = LOADS // members
+    layers = width // LOADS
+    block = own * layers
+    last_step = COUPLED * SUBSTEPS - 1
+    f32, bf16, i16, i32 = jnp.float32, jnp.bfloat16, jnp.int16, jnp.int32
+    col = lax.axis_index("tcol")
+    row = lax.axis_index("group") * trow_count + lax.axis_index("trow")
+    z = col // PAIR
+    me = row * PAIR + lax.rem(col, PAIR)
+
+    def device(depth, member):
+        return dict(
+            row_device(member // PAIR, trow_count), tcol=depth * PAIR + lax.rem(member, PAIR)
+        )
+
+    def member_of(d):
+        return lax.rem(me + d, members)
+
+    def depth_of(d):
+        return lax.rem(z + d, depth_count)
+
+    def each(first, last, action):
+        @pl.loop(first, last)
+        def _(d):
+            action(d)
+
+    barrier = pltpu.get_barrier_semaphore()
+
+    @pl.loop(1, total)
+    def _(d):
+        to = device(depth_of(d // members), member_of(lax.rem(d, members)))
+        pl.semaphore_signal(barrier, inc=1, device_id=to, device_id_type=MESH)
+
+    v_load = pltpu.make_async_copy(v_hbm, v_raw, load_sem.at[0])
+    u_load = pltpu.make_async_copy(u_hbm, u_raw, load_sem.at[1])
+    v_load.start()
+    u_load.start()
+
+    def iota(size, axis):
+        return lax.broadcasted_iota(i32, size, axis)
+
+    def ones_where(mask):
+        return jnp.where(mask, 1.0, 0.0).astype(bf16)
+
+    def dot(a, b):
+        return jnp.dot(a, b, preferred_element_type=f32)
+
+    def dot_turned(a, b):
+        return lax.dot_general(a, b, (((1,), (1,)), ((), ())), preferred_element_type=f32)
+
+    def lane_of(line):
+        member, inner = line // block, line % block
+        return (inner // own) * LOADS + member * own + inner % own
+
+    square = (width, width)
+    line, column = iota(square, 0), iota(square, 1)
+    perm[0:width, :] = ones_where(lane_of(line) == column)
+    turn[...] = ones_where(lane_of(column) == line)
+    outer = (LOADS, width)
+    perm[width : width + LOADS, :] = ones_where(
+        (layers - 1) * LOADS + iota(outer, 0) == iota(outer, 1)
+    )
+    eye[...] = ones_where(iota((count, count), 0) == iota((count, count), 1))
+
+    src, dst = iota((count, count), 0), iota((count, count), 1)
+    src_a, src_b, dst_a, dst_b = src % height, src // height, dst % height, dst // height
+
+    def taps(distance, mask):
+        value = jnp.where(distance == 3, -2.0, jnp.where((distance == 1) | (distance == 2), -1.0, 0.0))
+        return jnp.where(mask, value, 0.0)
+
+    same_a, same_b = src_a == dst_a, src_b == dst_b
+    stencil[0:count, :] = (
+        jnp.where(src == dst, 16.0, 0.0)
+        + taps(jnp.abs(src_b - dst_b), same_a)
+        + taps(jnp.abs(src_a - dst_a), same_b)
+    ).astype(bf16)
+    stencil[count : 2 * count, :] = (
+        taps(dst_a + height - src_a, same_b) + taps(src_a + height - dst_a, same_b)
+    ).astype(bf16)
+    stencil[2 * count : 3 * count, :] = (
+        taps(dst_b + breadth - src_b, same_a) + taps(src_b + breadth - dst_b, same_a)
+    ).astype(bf16)
+    node_a = iota((16, count), 1) % height
+    edges[0] = ones_where(node_a >= height - REACH)
+    edges[1] = ones_where(node_a < REACH)
+
+    spread = ones_where(iota((height, count), 0) == iota((height, count), 1) % height).astype(f32)
+    wide = jnp.dot(stiff_ref[...], spread, precision=HIGHEST, preferred_element_type=f32)
+    own_b = iota((breadth, count), 0) == iota((breadth, count), 1) // height
+    places[0:3, :] = position_ref[...]
+    places[3:8, :] = jnp.zeros((5, points), f32)
+    facts_out[0:3, :] = position_ref[...]
+    facts_out[3:6, :] = normal_ref[...] * (area_ref[...] * (1.0 / SPHERE_AREA))
+    facts_out[6:9, :] = normal_ref[...]
+    numbers = map_ref[...]
+    facts_out[9:10, :] = ((numbers % breadth) * height + numbers // breadth).astype(f32)
+    facts_out[10:11, :] = jnp.sum(jnp.where(own_b, wide, 0.0), axis=0, keepdims=True)
+    facts_out[13:16, :] = jnp.zeros((3, points), f32)
+    targets[z] = places[...]
+
+    halves[:, :, 0] = jnp.zeros((2, parts) + halves.shape[3:], bf16)
+    halves[:, :, row_count + 1] = jnp.zeros((2, parts) + halves.shape[3:], bf16)
+    beyond = halo_in.shape[:3] + (row_count, block, half)
+    halo_in[:, :, :, :, block : 2 * block, :] = jnp.zeros(beyond, bf16)
+    present = (z > 0, z < depth_count - 1)
+    for side in range(2):
+
+        @pl.when(jnp.logical_not(present[side]))
+        def _():
+            halo_in[:, :, side, :, 0:block, :] = jnp.zeros(beyond[:2] + beyond[3:], bf16)
+
+    def plane_copy(d, source, target, send, recv):
+        return pltpu.make_async_remote_copy(
+            src_ref=source, dst_ref=target.at[me], send_sem=send.at[d], recv_sem=recv.at[d],
+            device_id=device(z, member_of(d)), device_id_type=MESH,
+        )
+
+    def facts_copy(d):
+        return plane_copy(d, facts_out, facts, facts_send, facts_recv)
+
+    def places_copy(d):
+        return pltpu.make_async_remote_copy(
+            src_ref=places, dst_ref=targets.at[z],
+            send_sem=places_send.at[d], recv_sem=places_recv.at[d],
+            device_id=device(depth_of(d), me), device_id_type=MESH,
+        )
+
+    def first_copy(d):
+        return plane_copy(d, first_out, first_in, first_send, first_recv)
+
+    def in_copy(d):
+        return plane_copy(d, in_out.at[member_of(d)], in_in, in_send, in_recv)
+
+    def speed_copy(d):
+        return plane_copy(d, speed_out, speed_in, speed_send, speed_recv)
+
+    def final_copy(part, d):
+        return plane_copy(
+            d, final_out.at[part, member_of(d)], final_in.at[part],
+            final_send.at[part], final_recv.at[part],
+        )
+
+    def scale_copy(part, d):
+        return plane_copy(
+            d, scale_out.at[part], scale_in.at[part], scale_send.at[part], scale_recv.at[part]
+        )
+
+    def part_copy(repeat, dz, dj):
+        lines = pl.ds(pl.multiple_of(member_of(dj) * own, own), own)
+        return pltpu.make_async_remote_copy(
+            src_ref=part_out.at[repeat, depth_of(dz), lines, :],
+            dst_ref=part_in.at[repeat, z, me],
+            send_sem=part_send.at[repeat, dz, dj], recv_sem=part_recv.at[repeat, dz, dj],
+            device_id=device(depth_of(dz), member_of(dj)), device_id_type=MESH,
+        )
+
+    def halo_copy(step, part, side, arriving):
+        there = side if arriving else 1 - side
+        step_z = jnp.maximum(z - 1, 0) if side == 0 else jnp.minimum(z + 1, depth_count - 1)
+        return pltpu.make_async_remote_copy(
+            src_ref=halo_out.at[step, part, side],
+            dst_ref=halo_in.at[step, part, there, :, 0:block, :],
+            send_sem=halo_send.at[step, part, side], recv_sem=halo_recv.at[step, part, there],
+            device_id=device(step_z, me), device_id_type=MESH,
+        )
+
+    def as_column(value):
+        return jnp.broadcast_to(value, (half, value.shape[1])).T
+
+    def one_hot(s):
+        onehot[s] = ones_where(iota((count, points), 0).astype(f32) == facts[s, 9:10, :])
+
+    def one_hot_back(s):
+        nodes = as_column(facts[s, 9:10, :])
+        for lanes in range(2):
+            numbers = (iota((points, half), 1) + lanes * half).astype(f32)
+            onehot_back[s, :, lanes * half : (lanes + 1) * half] = ones_where(numbers == nodes)
+
+    facts[me] = facts_out[...]
+    one_hot(me)
+
+    def largest(value):
+        reduced = jnp.max(jnp.abs(value), axis=0)
+        top = jnp.max(jnp.max(reduced, axis=1, keepdims=True), axis=0, keepdims=True)
+        return jnp.maximum(top, 1e-30)
+
+    def split(value):
+        high = value.astype(bf16).astype(f32)
+        return jnp.concatenate([high, value - high], axis=-2).astype(bf16)
+
+    def turned(raw, part, inverse, lines):
+        rows = []
+        for j in range(breadth):
+            picks = [
+                raw[part, pl.ds(lanes * breadth + j, height, stride=2 * breadth), :]
+                for lanes in range(2)
+            ]
+            rows.append(jnp.concatenate(picks, axis=1))
+        value = jnp.round(jnp.concatenate(rows, axis=0) * inverse)
+        high = jnp.round(value * (1.0 / 256.0))
+        low = value - 256.0 * high
+        return (
+            dot_turned(perm[0:lines, :], high.astype(bf16)),
+            dot_turned(perm[0:lines, :], low.astype(bf16)),
+        )
+
+    def top_of(raw):
+        return largest(raw[...].reshape(raw.shape[0] * raw.shape[1] // 8, 8, half))
+
+    v_load.wait()
+    v_top = top_of(v_raw)
+    v_scale, v_inverse = v_top * (1.0 / LEVELS), LEVELS / v_top
+    facts_out[12:13, :] = jnp.broadcast_to(v_scale, (1, points))
+    picked_all = jnp.zeros((LOADS, points), f32)
+    for part in range(parts):
+        high, low = turned(v_raw, part, v_inverse, width + LOADS)
+        whole = high[0:width] * 256.0 + low[0:width]
+        in_out[:, part, block : 2 * block, :] = (
+            whole.reshape(members, block, count).astype(i32).astype(i16)
+        )
+        rows = jnp.concatenate([high[width:], low[width:]], axis=0).astype(bf16)
+        both = dot(rows, onehot[me])
+        picked = both[0:LOADS] * 256.0 + both[LOADS:]
+        picked_all = picked_all + picked * (normal_ref[part : part + 1, :] * v_scale)
+    own_speed[...] = picked_all
+    first_out[...] = picked_all.astype(bf16)
+    first_in[me] = first_out[...]
+
+    u_load.wait()
+    u_top = top_of(u_raw)
+    u_scale, u_inverse = u_top * (1.0 / LEVELS), LEVELS / u_top
+    facts_out[11:12, :] = jnp.broadcast_to(u_scale, (1, points))
+    facts[me] = facts_out[...]
+    for part in range(parts):
+        high, low = turned(u_raw, part, u_inverse, width)
+        whole = high * 256.0 + low
+        in_out[:, part, 0:block, :] = whole.reshape(members, block, count).astype(i32).astype(i16)
+    in_in[me] = in_out[me]
+
+    pl.semaphore_wait(barrier, total - 1)
+    each(1, members, lambda d: facts_copy(d).start())
+    each(1, depth_count, lambda d: places_copy(d).start())
+    each(1, members, lambda d: first_copy(d).start())
+    each(1, members, lambda d: in_copy(d).start())
+
+    each(1, members, lambda d: facts_copy(d).wait_recv())
+
+    @pl.loop(0, members)
+    def _(s):
+        for k in range(6):
+            source_cols[s, k] = as_column(facts[s, k : k + 1, :])
+
+    group = 32
+
+    def tile(depth):
+        def blocks(index, carry):
+            source = index // (points // half)
+            lanes = pl.ds(pl.multiple_of(lax.rem(index, points // half) * half, half), half)
+            known = [targets[depth, k : k + 1, lanes] for k in range(3)]
+
+            def rows_of(g, inner):
+                start = pl.multiple_of(g * group, group)
+                rows = pl.ds(start, group)
+                dx = known[0] - source_cols[source, 0, rows, :]
+                dy = known[1] - source_cols[source, 1, rows, :]
+                dz = known[2] - source_cols[source, 2, rows, :]
+                numerator = (
+                    source_cols[source, 3, rows, :] * dx
+                    + source_cols[source, 4, rows, :] * dy
+                    + source_cols[source, 5, rows, :] * dz
+                )
+                squared = dx * dx + dy * dy + dz * dz + SMOOTHING * SMOOTHING
+                inverse = lax.rsqrt(squared)
+                value = numerator * inverse * (inverse * inverse)
+                deep = pl.ds(pl.multiple_of(source * points + start, group), group)
+                tiles[depth, deep, lanes] = value.astype(bf16)
+                return inner
+
+            return lax.fori_loop(0, points // group, rows_of, carry, unroll=2)
+
+        lax.fori_loop(0, members * (points // half), blocks, 0)
+
+    def send_pressures(repeat, speeds):
+        @pl.loop(1, depth_count + 1)
+        def _(d):
+            depth = depth_of(d)
+            if repeat == 0:
+
+                @pl.when(d < depth_count)
+                def _():
+                    places_copy(depth_count - d).wait_recv()
+
+                tile(depth)
+
+                @pl.when(d == 1)
+                def _():
+                    each(1, members, lambda d: first_copy(d).wait_recv())
+
+            value = dot(speeds(), tiles[depth])
+            if repeat == 0:
+                value = value + jnp.where(depth == z, 0.5, 0.0) * own_speed[...]
+            part_out[repeat, depth] = value
+
+            @pl.when(d < depth_count)
+            def _():
+                each(0, members, lambda dj: part_copy(repeat, d, dj).start())
+
+            @pl.when(d == depth_count)
+            def _():
+                each(1, members, lambda dj: part_copy(repeat, 0, dj).start())
+
+        part_in[repeat, z, me] = part_out[
+            repeat, z, pl.ds(pl.multiple_of(me * own, own), own), :
+        ]
+
+    def parts_taken(repeat, action):
+        each(1, members, lambda dj: action(part_copy(repeat, 0, dj)))
+
+        @pl.loop(1, depth_count)
+        def _(d):
+            each(0, members, lambda dj: action(part_copy(repeat, d, dj)))
+
+    def interior(part, now):
+        def view(dr):
+            return halves[now, part, pl.ds(1 + dr, row_count)]
+
+        def rows16(value):
+            return value.reshape(members * 2 * block // 16, 16, count)
+
+        down = rows16(view(-1)) * edges[0] + rows16(view(1)) * edges[1]
+        flat = (members * 2 * block, count)
+        lines = jnp.concatenate([view(0).reshape(flat), down.reshape(flat)], axis=1)
+        summed[part] = dot(lines, stencil[0 : 2 * count, :])
+
+    def send_halos(step, part):
+        for side in range(2):
+
+            @pl.when(present[side])
+            def _():
+                halo_copy(step, part, side, False).start()
+
+    def place_halo(step, part, r, x, value):
+        lanes = x * half
+        halo_out[step, part, x, r] = value[:, lanes : lanes + half].astype(bf16)
+
+    send_pressures(
+        0, lambda: jnp.concatenate([first_in[s] for s in range(members)], axis=1)
+    )
+
+    @pl.loop(0, members, unroll=2)
+    def _(s):
+        one_hot(s)
+        one_hot_back(s)
+        stiff_now[s] = jnp.broadcast_to(facts[s, 10:11, :] * (-TIME_STEP / 12.0), (8, count))
+
+    each(1, members, lambda d: in_copy(d).wait_recv())
+
+    @pl.loop(0, parts)
+    def _(part):
+        @pl.loop(0, row_count)
+        def _(r):
+            for x in range(PAIR):
+                s = r * PAIR + x
+                value = in_in[s, part].astype(i32).astype(f32)
+                u_new = value[0:block] * facts[s, 11:12, :]
+                u_now[part, s] = u_new
+                v_now[part, s] = value[block : 2 * block] * facts[s, 12:13, :]
+                halves[0, part, 1 + r, x] = split(u_new)
+                place_halo(0, part, r, x, u_new)
+
+        send_halos(0, part)
+        interior(part, 0)
+
+    def take_pressures(repeat):
+        parts_taken(repeat, lambda copy: copy.wait_recv())
+
+        @pl.loop(0, members, unroll=4)
+        def _(s):
+            value = part_in[repeat, 0, s]
+            for d in range(1, depth_count):
+                value = value + part_in[repeat, d, s]
+            if repeat > 0:
+                value = value + 0.5 * spoken[s]
+            pieces = [
+                split(value * (facts[s, 6 + k : 7 + k, :] * (-TIME_STEP))) for k in range(parts)
+            ]
+            both = dot(jnp.concatenate(pieces, axis=0), onehot_back[s])
+            for k in range(parts):
+                load[k, s] = both[16 * k : 16 * k + 8] + both[16 * k + 8 : 16 * k + 16]
+
+    def advance(part, step, final):
+        now = lax.rem(step, 2)
+        later = 1 - now
+        for side in range(2):
+
+            @pl.when(present[side])
+            def _():
+                halo_copy(step, part, side, True).wait_recv()
+
+        inner = pl.ds(1, row_count)
+        flat = (members * 2 * block, half)
+        low = jnp.stack(
+            [halves[now, part, inner, 1, :, 0:half], halo_in[step, part, 1]], axis=1
+        ).reshape(flat)
+        high = jnp.stack(
+            [halo_in[step, part, 0], halves[now, part, inner, 0, :, half : 2 * half]], axis=1
+        ).reshape(flat)
+        beside[...] = dot(jnp.concatenate([low, high], axis=1), stencil[2 * count : 3 * count, :])
+
+        @pl.loop(0, row_count)
+        def _(r):
+            for x in range(PAIR):
+                s = r * PAIR + x
+                band = pl.ds(pl.multiple_of(s * 2 * block, 2 * block), 2 * block)
+                both = summed[part, band, :] + beside[band, :]
+                plane = (both[0:block] + both[block : 2 * block]).reshape(layers, own, count)
+                u_old = u_now[part, s].reshape(layers, own, count)
+                under = jnp.concatenate([u_old[0:1], u_old[: layers - 1]], axis=0)
+                above = jnp.concatenate([u_old[1:], u_old[layers - 1 :]], axis=0)
+                v_new = (
+                    v_now[part, s].reshape(layers, own, count)
+                    + stiff_now[s] * plane
+                    - (TIME_STEP * THICKNESS) * (2.0 * u_old - under - above)
+                )
+                v_new = jnp.concatenate(
+                    [v_new[: layers - 1], v_new[layers - 1 :] + load[part, s]], axis=0
+                )
+                u_new = (u_old + TIME_STEP * v_new).reshape(block, count)
+                v_now[part, s] = v_new.reshape(block, count)
+                u_now[part, s] = u_new
+                if not final:
+                    halves[later, part, 1 + r, x] = split(u_new)
+                    place_halo(step + 1, part, r, x, u_new)
+
+        if not final:
+            send_halos(step + 1, part)
+            interior(part, later)
+
+    take_pressures(0)
+
+    @pl.loop(0, SUBSTEPS)
+    def _(step):
+        @pl.loop(0, parts)
+        def _(part):
+            advance(part, step, False)
+
+    spoken_rows = []
+    for s in range(members):
+        pieces = [split(v_now[k, s, block - own : block]) for k in range(parts)]
+        both = dot(jnp.concatenate(pieces, axis=0), onehot[s])
+        value = jnp.zeros((own, points), f32)
+        for k in range(parts):
+            value = value + facts[s, 6 + k : 7 + k, :] * (
+                both[16 * k : 16 * k + 8] + both[16 * k + 8 : 16 * k + 16]
+            )
+        spoken[s] = value
+        spoken_rows.append(value)
+    pairs = members // 2
+    speed_out[...] = jnp.concatenate(
+        [
+            jnp.concatenate(spoken_rows[:pairs], axis=1),
+            jnp.concatenate(spoken_rows[pairs:], axis=1),
+        ], axis=0
+    ).astype(bf16)
+    each(1, members, lambda d: speed_copy(d).start())
+    speed_in[me] = speed_out[...]
+    each(1, members, lambda d: speed_copy(d).wait_recv())
+
+    def gathered():
+        arrived = [speed_in[s].astype(f32) for s in range(members)]
+        lower = jnp.concatenate([value[0:own] for value in arrived], axis=0)
+        upper = jnp.concatenate([value[own : 2 * own] for value in arrived], axis=0)
+        return jnp.concatenate([lower, upper], axis=1).astype(bf16)
+
+    send_pressures(1, gathered)
+    take_pressures(1)
+
+    @pl.loop(SUBSTEPS, last_step)
+    def _(step):
+        @pl.loop(0, parts)
+        def _(part):
+            advance(part, step, False)
+
+    @pl.loop(0, parts)
+    def _(part):
+        advance(part, last_step, True)
+        for f, state in enumerate((u_now, v_now)):
+            value = state[part]
+            high = largest(value.reshape(members * layers, own, count))
+            scale_out[part, :, f * (half // 2) : (f + 1) * (half // 2)] = jnp.broadcast_to(
+                high * (1.0 / LEVELS), (1, half // 2)
+            )
+            whole = jnp.round(value * (LEVELS / high))
+            final_out[part, :, f * block : (f + 1) * block, :] = whole.astype(i32).astype(i16)
+        each(1, members, lambda d: final_copy(part, d).start())
+        each(1, members, lambda d: scale_copy(part, d).start())
+        final_in[part, me] = final_out[part, me]
+        scale_in[part, me] = scale_out[part]
+
+    @pl.loop(0, parts)
+    def _(part):
+        each(1, members, lambda d: final_copy(part, d).wait_recv())
+        each(1, members, lambda d: scale_copy(part, d).wait_recv())
+        value = final_in[part].astype(i32).astype(f32)
+        for f, result in enumerate((u_out, v_out)):
+            scale = scale_in[part, :, :, f * (half // 2) : f * (half // 2) + 1]
+            rows = (value[:, f * block : (f + 1) * block] * scale).reshape(width, count)
+            high = rows.astype(bf16)
+            low = (rows - high.astype(f32)).astype(bf16)
+            ordered = [dot(turn[...], piece).astype(bf16) for piece in (high, low)]
+            back = dot_turned(eye[...], ordered[0]) + dot_turned(eye[...], ordered[1])
+            for j in range(breadth):
+                for lanes in range(2):
+                    lines = pl.ds(lanes * breadth + j, height, stride=2 * breadth)
+                    result[part, lines, :] = back[
+                        j * height : (j + 1) * height, lanes * half : (lanes + 1) * half
+                    ]
+
+    each(1, members, lambda d: facts_copy(d).wait_send())
+    each(1, depth_count, lambda d: places_copy(d).wait_send())
+    each(1, members, lambda d: first_copy(d).wait_send())
+    each(1, members, lambda d: in_copy(d).wait_send())
+    each(1, members, lambda d: speed_copy(d).wait_send())
+    for repeat in range(COUPLED):
+        parts_taken(repeat, lambda copy: copy.wait_send())
+
+    @pl.loop(0, parts)
+    def _(part):
+        each(1, members, lambda d: final_copy(part, d).wait_send())
+        each(1, members, lambda d: scale_copy(part, d).wait_send())
+
+        @pl.loop(0, last_step + 1)
+        def _(step):
+            for side in range(2):
+
+                @pl.when(present[side])
+                def _():
+                    halo_copy(step, part, side, False).wait_send()
+
+
+def plane_on_device(shape, displacement, velocity, stiffness, wet_position, wet_normal, wet_area, wet_map):
+    col_count, row_count, _ = shape
+    depth_count = col_count // PAIR
+    members = row_count * PAIR
+    parts, height, breadth, width = displacement.shape
+    half = width // 2
+    points = wet_map.shape[0]
+    count = height * breadth
+    own = LOADS // members
+    block = own * (width // LOADS)
+    steps = COUPLED * SUBSTEPS
+    f32, bf16, i16 = jnp.float32, jnp.bfloat16, jnp.int16
+    dma = pltpu.SemaphoreType.DMA
+
+    def separated(state):
+        tiled = state.reshape(parts, height, breadth, 2, half).transpose(0, 1, 3, 2, 4)
+        return tiled.reshape(parts, height * 2 * breadth, half)
+
+    def joined(state):
+        tiled = state.reshape(parts, height, 2, breadth, half).transpose(0, 1, 3, 2, 4)
+        return tiled.reshape(parts, height, breadth, width)
+
+    raw = (parts, height * 2 * breadth, half)
+    state = jax.ShapeDtypeStruct(raw, f32)
+    field = VMEM((parts, members, block, count), f32)
+    anywhere = pl.BlockSpec(memory_space=pl.ANY)
+    slab = (members, parts, 2 * block, count)
+    final = (parts, members, 2 * block, count)
+    u_new, v_new = pl.pallas_call(
+        functools.partial(plane_kernel, shape),
+        out_shape=(state, state),
+        in_specs=[anywhere] * 2 + [whole_spec()] * 5,
+        out_specs=(whole_spec(), whole_spec()),
+        scratch_shapes=[
+            VMEM(raw, f32),
+            VMEM(raw, f32),
+            VMEM((width + LOADS, width), bf16),
+            VMEM((width, width), bf16),
+            VMEM((count, count), bf16),
+            VMEM((3 * count, count), bf16),
+            VMEM((2, 16, count), bf16),
+            VMEM(slab, i16),
+            VMEM(slab, i16),
+            VMEM((16, points), f32),
+            VMEM((members, 16, points), f32),
+            VMEM((8, points), f32),
+            VMEM((depth_count, 8, points), f32),
+            VMEM((members, 6, points, half), f32),
+            VMEM((LOADS, points), bf16),
+            VMEM((members, LOADS, points), bf16),
+            VMEM((depth_count, members * points, points), bf16),
+            VMEM((COUPLED, depth_count, LOADS, points), f32),
+            VMEM((COUPLED, depth_count, members, own, points), f32),
+            VMEM((members, own, points), f32),
+            VMEM((members, count, points), bf16),
+            VMEM((members, points, count), bf16),
+            field,
+            field,
+            VMEM((parts, members, own, count), f32),
+            VMEM((2, parts, row_count + 2, PAIR, 2 * block, count), bf16),
+            VMEM((parts, members * 2 * block, count), f32),
+            VMEM((members * 2 * block, count), f32),
+            VMEM((members, 8, count), f32),
+            VMEM((LOADS, points), f32),
+            VMEM((steps, parts, 2, row_count, block, half), bf16),
+            VMEM((steps, parts, 2, row_count, 2 * block, half), bf16),
+            VMEM((2 * own, members // 2 * points), bf16),
+            VMEM((members, 2 * own, members // 2 * points), bf16),
+            VMEM(final, i16),
+            VMEM(final, i16),
+            VMEM((parts, 1, half), f32),
+            VMEM((parts, members, 1, half), f32),
+            dma((2,)),
+            dma((members,)),
+            dma((members,)),
+            dma((depth_count,)),
+            dma((depth_count,)),
+            dma((members,)),
+            dma((members,)),
+            dma((members,)),
+            dma((members,)),
+            dma((COUPLED, depth_count, members)),
+            dma((COUPLED, depth_count, members)),
+            dma((steps, parts, 2)),
+            dma((steps, parts, 2)),
+            dma((members,)),
+            dma((members,)),
+            dma((parts, members)),
+            dma((parts, members)),
+            dma((parts, members)),
+            dma((parts, members)),
+        ],
+        compiler_params=pltpu.CompilerParams(
+            collective_id=0, has_side_effects=True, vmem_limit_bytes=67043328
+        ),
+        name="plane_steps",
+    )(
+        separated(displacement), separated(velocity), stiffness.T, wet_position, wet_normal,
+        wet_area[None, :], wet_map[None, :],
+    )
+    return (joined(u_new), joined(v_new))
+
+
+def by_planes(shape, displacement, wet_map):
+    col_count, row_count, _ = shape
+    _, height, breadth, width = displacement.shape
+    members = row_count * PAIR
+    return (
+        col_count % PAIR == 0
+        and LOADS % members == 0
+        and LOADS // members == 8
+        and height * breadth == wet_map.shape[0] == width == 256
+    )
+
+
+def either(shape, *arrays):
+    chosen = plane_on_device if by_planes(shape, arrays[0], arrays[-1]) else on_device
+    return chosen(shape, *arrays)
+
+
 def solution(mesh):
     sizes = mesh.shape
     shape = (sizes["tcol"], sizes["group"] * sizes["trow"], sizes["trow"])
     state = P(None, ("group", "trow"), "tcol", None)
     wet = ("group", "trow", "tcol")
     return jax.shard_map(
-        functools.partial(on_device, shape),
+        functools.partial(either, shape),
         mesh=mesh,
         in_specs=(
             state,

time: 100 us -> 85.4 us (0.85)
  Pallas kernels: 94.1 us -> 81.5 us
  local copies, waits for them, and re-layouts: 4.44 us -> 3.02 us
    pallas_call x1, Pallas kernels: 94.1 us -> 81.5 us  [plane_on_device(): pl.pallas_call(functools.partial(plane_kernel, shape), out_shape=(state,...]
    unnamed x8 -> x4, local copies, waits for them, and re-layouts: 3.69 us -> 3.02 us
where the time goes in v2:
time: 85.4 us; the launch traced here: 85.2 us
  Pallas kernels  81.5 us (95%)
  local copies, waits for them, and re-layouts  3.02 us (4%)
    pallas_call x1, Pallas kernels, plane_on_device(): pl.pallas_call(functools.partial(plane_kernel, shape), out_shape=(state,...  81.5 us
    unnamed x4, local copies, waits for them, and re-layouts  3.02 us

profile of v2, /device:TPU:0, one launch (start us, length us, event | category | flops | bytes accessed | tf_op | source)
XLA Modules:
  0.0 85.2 jit_solution(3872207973726492418)
XLA Ops:
  0.6 81.5 %plane_steps.1 = (f32[3,512,128]{2,1,0:T(8,128)}, f32[3,512,128]{2,1,0:T(8,128)}) custom-call(f32[3,512,128]{2,1,0:T(8,128)} %bitcast.23, f32[3,512,128]{2,1,0:T(8,128)} %bitcast.24, f32[8,32]{1,0:T(8,128)} %bitcast.27, f32[3,256]{1,0:T(4,128)} %position_ref.1, f32[3,256]{1,0:T(4,128)} %normal_ref.1, f32[1,256]{1,0:T(1,128)} %bitcast.28, s32[1,256]{1,0:T(1,128)} %bitcast.29), custom_call_target="tpu_custom_call" | custom-call | tf_op jit(solution)/shard_map/plane_steps/pallas_call | solution.py:1073
  82.1 0.0 copy-start
  82.2 2.1 %copy.11 = f32[3,32,8,256]{3,2,1,0:T(8,128)} copy(f32[3,32,8,256]{3,2,1,0:T(8,128)} %bitcast.26) | data formatting | bytes 1572864
  84.3 0.0 copy-done
  84.3 0.9 %copy.12 = f32[3,32,8,256]{3,2,1,0:T(8,128)} copy(f32[3,32,8,256]{3,2,1,0:T(8,128)S(1)} %bitcast.25) | data formatting | bytes 1572864
Async XLA Ops:
  82.1 2.1 %copy-start = (f32[3,512,128]{2,1,0:T(8,128)S(1)}, f32[3,512,128]{2,1,0:T(8,128)}, u32[]{:S(2)}) copy-start(f32[3,512,128]{2,1,0:T(8,128)} %get-tuple-element.5) | copy-start | bytes 2359300

commit v3 on v2

--- a/solution.py
+++ b/solution.py
@@ -485,9 +485,9 @@
 
 def plane_kernel(
     shape, u_hbm, v_hbm, stiff_ref, position_ref, normal_ref, area_ref, map_ref, u_out, v_out,
-    u_raw, v_raw, perm, turn, eye, stencil, edges, in_out, in_in, facts_out, facts, places, targets,
+    u_raw, v_raw, perm, turn, eye, stencil, in_out, in_in, facts_out, facts, places, targets,
     source_cols, first_out, first_in, tiles, part_out, part_in, spoken,
-    onehot, onehot_back, u_now, v_now, load, halves, summed, beside, stiff_now, own_speed,
+    onehot, onehot_back, u_now, v_now, load, halves, summed, patched, stiff_now, own_speed,
     halo_out, halo_in, speed_out, speed_in, final_out, final_in, scale_out, scale_in,
     load_sem, facts_send, facts_recv, places_send, places_recv, first_send, first_recv,
     in_send, in_recv, part_send, part_recv, halo_send, halo_recv, speed_send, speed_recv,
@@ -504,6 +504,7 @@
     own = LOADS // members
     layers = width // LOADS
     block = own * layers
+    columns = PAIR * breadth
     last_step = COUPLED * SUBSTEPS - 1
     f32, bf16, i16, i32 = jnp.float32, jnp.bfloat16, jnp.int16, jnp.int32
     col = lax.axis_index("tcol")
@@ -566,27 +567,10 @@
     eye[...] = ones_where(iota((count, count), 0) == iota((count, count), 1))
 
     src, dst = iota((count, count), 0), iota((count, count), 1)
-    src_a, src_b, dst_a, dst_b = src % height, src // height, dst % height, dst // height
-
-    def taps(distance, mask):
-        value = jnp.where(distance == 3, -2.0, jnp.where((distance == 1) | (distance == 2), -1.0, 0.0))
-        return jnp.where(mask, value, 0.0)
-
-    same_a, same_b = src_a == dst_a, src_b == dst_b
-    stencil[0:count, :] = (
-        jnp.where(src == dst, 16.0, 0.0)
-        + taps(jnp.abs(src_b - dst_b), same_a)
-        + taps(jnp.abs(src_a - dst_a), same_b)
-    ).astype(bf16)
-    stencil[count : 2 * count, :] = (
-        taps(dst_a + height - src_a, same_b) + taps(src_a + height - dst_a, same_b)
-    ).astype(bf16)
-    stencil[2 * count : 3 * count, :] = (
-        taps(dst_b + breadth - src_b, same_a) + taps(src_b + breadth - dst_b, same_a)
-    ).astype(bf16)
-    node_a = iota((16, count), 1) % height
-    edges[0] = ones_where(node_a >= height - REACH)
-    edges[1] = ones_where(node_a < REACH)
+    distance = jnp.abs(src - dst)
+    taps = jnp.where(distance == 3, -2.0, jnp.where(distance < 3, -1.0, 0.0))
+    taps = jnp.where(distance == 0, 16.0, taps)
+    stencil[...] = jnp.where(src // half == dst // half, taps, 0.0).astype(bf16)
 
     spread = ones_where(iota((height, count), 0) == iota((height, count), 1) % height).astype(f32)
     wide = jnp.dot(stiff_ref[...], spread, precision=HIGHEST, preferred_element_type=f32)
@@ -602,16 +586,12 @@
     facts_out[13:16, :] = jnp.zeros((3, points), f32)
     targets[z] = places[...]
 
-    halves[:, :, 0] = jnp.zeros((2, parts) + halves.shape[3:], bf16)
-    halves[:, :, row_count + 1] = jnp.zeros((2, parts) + halves.shape[3:], bf16)
-    beyond = halo_in.shape[:3] + (row_count, block, half)
-    halo_in[:, :, :, :, block : 2 * block, :] = jnp.zeros(beyond, bf16)
     present = (z > 0, z < depth_count - 1)
-    for side in range(2):
+    for side, first in ((0, 0), (1, columns + REACH)):
 
         @pl.when(jnp.logical_not(present[side]))
         def _():
-            halo_in[:, :, side, :, 0:block, :] = jnp.zeros(beyond[:2] + beyond[3:], bf16)
+            u_now[:, :, first : first + REACH] = jnp.zeros((2, parts, REACH, block, half), f32)
 
     def plane_copy(d, source, target, send, recv):
         return pltpu.make_async_remote_copy(
@@ -663,13 +643,37 @@
         step_z = jnp.maximum(z - 1, 0) if side == 0 else jnp.minimum(z + 1, depth_count - 1)
         return pltpu.make_async_remote_copy(
             src_ref=halo_out.at[step, part, side],
-            dst_ref=halo_in.at[step, part, there, :, 0:block, :],
+            dst_ref=halo_in.at[step, part, there],
             send_sem=halo_send.at[step, part, side], recv_sem=halo_recv.at[step, part, there],
             device_id=device(step_z, me), device_id_type=MESH,
         )
 
     def as_column(value):
         return jnp.broadcast_to(value, (half, value.shape[1])).T
+
+    bunch = iota((8, half), 1) // height
+    upper_half, odd = bunch >= 2, bunch % 2 == 1
+
+    def exchange(values):
+        rows = values[0].shape[0]
+
+        def choose(mask, a, b):
+            shape3 = (rows // 8, 8, half)
+            return jnp.where(mask, b.reshape(shape3), a.reshape(shape3)).reshape(rows, half)
+
+        def rolled(value, bunches):
+            return pltpu.roll(value, bunches * height, 1)
+
+        lows = [choose(upper_half, values[i], rolled(values[i + 2], 2)) for i in range(2)]
+        highs = [choose(upper_half, rolled(values[i], 2), values[i + 2]) for i in range(2)]
+        result = []
+        for first, second in (lows, highs):
+            result.append(choose(odd, first, rolled(second, 1)))
+            result.append(choose(odd, rolled(first, 3), second))
+        return result
+
+    def tile_lanes(t):
+        return slice(t * half, (t + 1) * half)
 
     def one_hot(s):
         onehot[s] = ones_where(iota((count, points), 0).astype(f32) == facts[s, 9:10, :])
@@ -825,16 +829,8 @@
             each(0, members, lambda dj: action(part_copy(repeat, d, dj)))
 
     def interior(part, now):
-        def view(dr):
-            return halves[now, part, pl.ds(1 + dr, row_count)]
-
-        def rows16(value):
-            return value.reshape(members * 2 * block // 16, 16, count)
-
-        down = rows16(view(-1)) * edges[0] + rows16(view(1)) * edges[1]
-        flat = (members * 2 * block, count)
-        lines = jnp.concatenate([view(0).reshape(flat), down.reshape(flat)], axis=1)
-        summed[part] = dot(lines, stencil[0 : 2 * count, :])
+        lines = halves[now, part].reshape(columns // 2 * 2 * block, 2 * half)
+        summed[part] = dot(lines, stencil[...])
 
     def send_halos(step, part):
         for side in range(2):
@@ -843,9 +839,18 @@
             def _():
                 halo_copy(step, part, side, False).start()
 
-    def place_halo(step, part, r, x, value):
-        lanes = x * half
-        halo_out[step, part, x, r] = value[:, lanes : lanes + half].astype(bf16)
+    def place(step, part, later, pair, j, value):
+        c = pair * 2 + j
+        u_now[later, part, REACH + c] = value
+        high = value.astype(bf16)
+        halves[later, part, pair, 0:block, tile_lanes(j)] = high
+        halves[later, part, pair, block : 2 * block, tile_lanes(j)] = (
+            value - high.astype(f32)
+        ).astype(bf16)
+        if isinstance(c, int):
+            for side, first in ((0, 0), (1, columns - REACH)):
+                if first <= c < first + REACH:
+                    halo_out[step, part, side, c - first] = high
 
     send_pressures(
         0, lambda: jnp.concatenate([first_in[s] for s in range(members)], axis=1)
@@ -855,23 +860,33 @@
     def _(s):
         one_hot(s)
         one_hot_back(s)
-        stiff_now[s] = jnp.broadcast_to(facts[s, 10:11, :] * (-TIME_STEP / 12.0), (8, count))
+
+    for x in range(PAIR):
+        for t in range(breadth // 4):
+            given = [
+                jnp.broadcast_to(facts[r * PAIR + x, 10:11, tile_lanes(t)], (8, half))
+                for r in range(row_count)
+            ]
+            for g, value in enumerate(exchange(given)):
+                stiff_now[x * breadth + t * 4 + g] = value * (-TIME_STEP / 12.0)
 
     each(1, members, lambda d: in_copy(d).wait_recv())
 
     @pl.loop(0, parts)
     def _(part):
-        @pl.loop(0, row_count)
-        def _(r):
-            for x in range(PAIR):
-                s = r * PAIR + x
-                value = in_in[s, part].astype(i32).astype(f32)
-                u_new = value[0:block] * facts[s, 11:12, :]
-                u_now[part, s] = u_new
-                v_now[part, s] = value[block : 2 * block] * facts[s, 12:13, :]
-                halves[0, part, 1 + r, x] = split(u_new)
-                place_halo(0, part, r, x, u_new)
-
+        for x in range(PAIR):
+            for t in range(breadth // 4):
+                given = []
+                for r in range(row_count):
+                    value = in_in[r * PAIR + x, part, :, tile_lanes(t)].astype(i32).astype(f32)
+                    scales = facts[r * PAIR + x, 11:13, tile_lanes(t)]
+                    given.append(jnp.concatenate(
+                        [value[0:block] * scales[0:1], value[block:] * scales[1:2]], axis=0
+                    ))
+                for g, value in enumerate(exchange(given)):
+                    c = x * breadth + t * 4 + g
+                    v_now[part, c] = value[block:]
+                    place(0, part, 0, c // 2, c % 2, value[0:block])
         send_halos(0, part)
         interior(part, 0)
 
@@ -889,55 +904,71 @@
                 split(value * (facts[s, 6 + k : 7 + k, :] * (-TIME_STEP))) for k in range(parts)
             ]
             both = dot(jnp.concatenate(pieces, axis=0), onehot_back[s])
-            for k in range(parts):
-                load[k, s] = both[16 * k : 16 * k + 8] + both[16 * k + 8 : 16 * k + 16]
+            patched[s] = jnp.concatenate(
+                [
+                    both[16 * k : 16 * k + 8] + both[16 * k + 8 : 16 * k + 16]
+                    for k in range(parts)
+                ], axis=0
+            )
+
+        for x in range(PAIR):
+            for t in range(breadth // 4):
+                given = [patched[r * PAIR + x, :, tile_lanes(t)] for r in range(row_count)]
+                for g, value in enumerate(exchange(given)):
+                    for k in range(parts):
+                        load[k, x * breadth + t * 4 + g] = value[own * k : own * (k + 1)]
 
     def advance(part, step, final):
         now = lax.rem(step, 2)
         later = 1 - now
-        for side in range(2):
+        for side, first in ((0, 0), (1, columns + REACH)):
 
             @pl.when(present[side])
             def _():
                 halo_copy(step, part, side, True).wait_recv()
-
-        inner = pl.ds(1, row_count)
-        flat = (members * 2 * block, half)
-        low = jnp.stack(
-            [halves[now, part, inner, 1, :, 0:half], halo_in[step, part, 1]], axis=1
-        ).reshape(flat)
-        high = jnp.stack(
-            [halo_in[step, part, 0], halves[now, part, inner, 0, :, half : 2 * half]], axis=1
-        ).reshape(flat)
-        beside[...] = dot(jnp.concatenate([low, high], axis=1), stencil[2 * count : 3 * count, :])
-
-        @pl.loop(0, row_count)
-        def _(r):
-            for x in range(PAIR):
-                s = r * PAIR + x
-                band = pl.ds(pl.multiple_of(s * 2 * block, 2 * block), 2 * block)
-                both = summed[part, band, :] + beside[band, :]
-                plane = (both[0:block] + both[block : 2 * block]).reshape(layers, own, count)
-                u_old = u_now[part, s].reshape(layers, own, count)
+                u_now[now, part, first : first + REACH] = halo_in[step, part, side].astype(f32)
+
+        def update(pair, start):
+            for j in range(2):
+                c = pair * 2 + j
+                both = summed[part, pl.ds(start, 2 * block), tile_lanes(j)]
+                plane = both[0:block] + both[block : 2 * block]
+
+                def near(offset):
+                    return u_now[now, part, REACH + c + offset]
+
+                beside = (near(-1) + near(1)) + (near(-2) + near(2))
+                beside = beside + 2.0 * (near(-3) + near(3))
+                plane = (plane - beside).reshape(layers, own, half)
+                u_old = near(0).reshape(layers, own, half)
                 under = jnp.concatenate([u_old[0:1], u_old[: layers - 1]], axis=0)
                 above = jnp.concatenate([u_old[1:], u_old[layers - 1 :]], axis=0)
                 v_new = (
-                    v_now[part, s].reshape(layers, own, count)
-                    + stiff_now[s] * plane
+                    v_now[part, c].reshape(layers, own, half)
+                    + stiff_now[c] * plane
                     - (TIME_STEP * THICKNESS) * (2.0 * u_old - under - above)
                 )
                 v_new = jnp.concatenate(
-                    [v_new[: layers - 1], v_new[layers - 1 :] + load[part, s]], axis=0
+                    [v_new[: layers - 1], v_new[layers - 1 :] + load[part, c]], axis=0
                 )
-                u_new = (u_old + TIME_STEP * v_new).reshape(block, count)
-                v_now[part, s] = v_new.reshape(block, count)
-                u_now[part, s] = u_new
-                if not final:
-                    halves[later, part, 1 + r, x] = split(u_new)
-                    place_halo(step + 1, part, r, x, u_new)
-
+                u_new = (u_old + TIME_STEP * v_new).reshape(block, half)
+                v_now[part, c] = v_new.reshape(block, half)
+                if final:
+                    u_now[later, part, REACH + c] = u_new
+                else:
+                    place(step + 1, part, later, pair, j, u_new)
+
+        edge = (REACH + 1) // 2
+        for pair in list(range(edge)) + list(range(columns // 2 - edge, columns // 2)):
+            update(pair, pair * 2 * block)
         if not final:
             send_halos(step + 1, part)
+
+        @pl.loop(edge, columns // 2 - edge, unroll=2)
+        def _(pair):
+            update(pair, pl.multiple_of(pair * 2 * block, 2 * block))
+
+        if not final:
             interior(part, later)
 
     take_pressures(0)
@@ -948,9 +979,20 @@
         def _(part):
             advance(part, step, False)
 
+    for x in range(PAIR):
+        for t in range(breadth // 4):
+            given = []
+            for g in range(4):
+                c = x * breadth + t * 4 + g
+                given.append(jnp.concatenate(
+                    [v_now[k, c, block - own : block] for k in range(parts)], axis=0
+                ))
+            for r, value in enumerate(exchange(given)):
+                patched[r * PAIR + x, :, tile_lanes(t)] = value
+
     spoken_rows = []
     for s in range(members):
-        pieces = [split(v_now[k, s, block - own : block]) for k in range(parts)]
+        pieces = [split(patched[s, own * k : own * (k + 1)]) for k in range(parts)]
         both = dot(jnp.concatenate(pieces, axis=0), onehot[s])
         value = jnp.zeros((own, points), f32)
         for k in range(parts):
@@ -988,14 +1030,20 @@
     @pl.loop(0, parts)
     def _(part):
         advance(part, last_step, True)
-        for f, state in enumerate((u_now, v_now)):
-            value = state[part]
-            high = largest(value.reshape(members * layers, own, count))
+        done = 1 - last_step % 2
+        for f, state in enumerate((u_now.at[done, part, pl.ds(REACH, columns)], v_now.at[part])):
+            high = largest(state[...].reshape(columns * layers, own, half))
             scale_out[part, :, f * (half // 2) : (f + 1) * (half // 2)] = jnp.broadcast_to(
                 high * (1.0 / LEVELS), (1, half // 2)
             )
-            whole = jnp.round(value * (LEVELS / high))
-            final_out[part, :, f * block : (f + 1) * block, :] = whole.astype(i32).astype(i16)
+            inverse = LEVELS / high
+            for x in range(PAIR):
+                for t in range(breadth // 4):
+                    given = [state[x * breadth + t * 4 + g] * inverse for g in range(4)]
+                    for r, value in enumerate(exchange(given)):
+                        final_out[
+                            part, r * PAIR + x, f * block : (f + 1) * block, tile_lanes(t)
+                        ] = jnp.round(value).astype(i32).astype(i16)
         each(1, members, lambda d: final_copy(part, d).start())
         each(1, members, lambda d: scale_copy(part, d).start())
         final_in[part, me] = final_out[part, me]
@@ -1066,7 +1114,7 @@
 
     raw = (parts, height * 2 * breadth, half)
     state = jax.ShapeDtypeStruct(raw, f32)
-    field = VMEM((parts, members, block, count), f32)
+    columns = PAIR * breadth
     anywhere = pl.BlockSpec(memory_space=pl.ANY)
     slab = (members, parts, 2 * block, count)
     final = (parts, members, 2 * block, count)
@@ -1081,8 +1129,7 @@
             VMEM((width + LOADS, width), bf16),
             VMEM((width, width), bf16),
             VMEM((count, count), bf16),
-            VMEM((3 * count, count), bf16),
-            VMEM((2, 16, count), bf16),
+            VMEM((count, count), bf16),
             VMEM(slab, i16),
             VMEM(slab, i16),
             VMEM((16, points), f32),
@@ -1098,16 +1145,16 @@
             VMEM((members, own, points), f32),
             VMEM((members, count, points), bf16),
             VMEM((members, points, count), bf16),
-            field,
-            field,
-            VMEM((parts, members, own, count), f32),
-            VMEM((2, parts, row_count + 2, PAIR, 2 * block, count), bf16),
-            VMEM((parts, members * 2 * block, count), f32),
-            VMEM((members * 2 * block, count), f32),
-            VMEM((members, 8, count), f32),
+            VMEM((2, parts, columns + 2 * REACH, block, half), f32),
+            VMEM((parts, columns, block, half), f32),
+            VMEM((parts, columns, own, half), f32),
+            VMEM((2, parts, columns // 2, 2 * block, 2 * half), bf16),
+            VMEM((parts, columns * block, 2 * half), f32),
+            VMEM((members, parts * own, count), f32),
+            VMEM((columns, 8, half), f32),
             VMEM((LOADS, points), f32),
-            VMEM((steps, parts, 2, row_count, block, half), bf16),
-            VMEM((steps, parts, 2, row_count, 2 * block, half), bf16),
+            VMEM((steps, parts, 2, REACH, block, half), bf16),
+            VMEM((steps, parts, 2, REACH, block, half), bf16),
             VMEM((2 * own, members // 2 * points), bf16),
             VMEM((members, 2 * own, members // 2 * points), bf16),
             VMEM(final, i16),
@@ -1135,11 +1182,13 @@
             dma((parts, members)),
         ],
         compiler_params=pltpu.CompilerParams(
-            collective_id=0, has_side_effects=True, vmem_limit_bytes=67043328
+            collective_id=0, has_side_effects=True, vmem_limit_bytes=48000000
         ),
         name="plane_steps",
     )(
-        separated(displacement), separated(velocity), stiffness.T, wet_position, wet_normal,
+        pltpu.with_memory_space_constraint(separated(displacement), pltpu.HBM),
+        pltpu.with_memory_space_constraint(separated(velocity), pltpu.HBM),
+        stiffness.T, wet_position, wet_normal,
         wet_area[None, :], wet_map[None, :],
     )
     return (joined(u_new), joined(v_new))
@@ -1154,6 +1203,8 @@
         and LOADS % members == 0
         and LOADS // members == 8
         and height * breadth == wet_map.shape[0] == width == 256
+        and row_count == 4
+        and height == 32
     )
 
 

time: 85.4 us -> 82.1 us (0.961)
  Pallas kernels: 81.5 us -> 77.4 us
    pallas_call x1, Pallas kernels: 81.5 us -> 77.4 us  [plane_on_device(): pl.pallas_call(functools.partial(plane_kernel, shape), out_shape=(state,...]
    unnamed x4 -> x12, local copies, waits for them, and re-layouts: 3.02 us -> 3.81 us
where the time goes in v3:
time: 82.1 us; the launch traced here: 81.8 us
  Pallas kernels  77.4 us (94%)
  local copies, waits for them, and re-layouts  3.81 us (5%)
    pallas_call x1, Pallas kernels, plane_on_device(): pl.pallas_call(functools.partial(plane_kernel, shape), out_shape=(state,...  77.4 us
    unnamed x12, local copies, waits for them, and re-layouts  3.81 us

profile of v3, /device:TPU:0, one launch (start us, length us, event | category | flops | bytes accessed | tf_op | source)
XLA Modules:
  0.0 81.8 jit_solution(2679659443768103283)
XLA Ops:
  0.6 0.0 copy-start.1
  0.6 0.0 copy-start
  0.7 0.0 copy-start.3
  0.7 0.7 copy-done.1
  1.3 0.0 copy-done
  1.3 0.0 copy-done.3
  1.3 0.0 copy-start.2
  1.3 0.7 copy-done.2
  2.0 0.0 copy-start.4
  2.0 0.7 copy-done.4
  2.7 77.4 %plane_steps.1 = (f32[3,512,128]{2,1,0:T(8,128)S(1)}, f32[3,512,128]{2,1,0:T(8,128)S(1)}) custom-call(f32[3,512,128]{2,1,0:T(8,128)} %bitcast.28, f32[3,512,128]{2,1,0:T(8,128)} %bitcast.29, f32[8,32]{1,0:T(8,128)S(1)} %bitcast.25, f32[3,256]{1,0:T(4,128)S(1)} %copy-done.1, f32[3,256]{1,0:T(4,128)S(1)} %copy-done.2, f32[1,256]{1,0:T(1,128)S(1)} %bitcast.26, ...), custom_call_target="tpu_custom_call" | custom-call | tf_op jit(solution)/shard_map/plane_steps/pallas_call | solution.py:1121
  80.1 0.9 %copy.11 = f32[3,32,8,256]{3,2,1,0:T(8,128)} copy(f32[3,32,8,256]{3,2,1,0:T(8,128)S(1)} %bitcast.24) | data formatting | bytes 1572864
  81.0 0.9 %copy.12 = f32[3,32,8,256]{3,2,1,0:T(8,128)} copy(f32[3,32,8,256]{3,2,1,0:T(8,128)S(1)} %bitcast.23) | data formatting | bytes 1572864
Async XLA Ops:
  0.6 0.7 copy-start.1
  0.6 0.7 copy-start
  0.7 0.7 copy-start.3
  1.3 0.7 copy-start.2
  2.0 0.7 copy-start.4

commit v4 on v3

--- a/solution.py
+++ b/solution.py
@@ -488,7 +488,7 @@
     u_raw, v_raw, perm, turn, eye, stencil, in_out, in_in, facts_out, facts, places, targets,
     source_cols, first_out, first_in, tiles, part_out, part_in, spoken,
     onehot, onehot_back, u_now, v_now, load, halves, summed, patched, stiff_now, own_speed,
-    halo_out, halo_in, speed_out, speed_in, final_out, final_in, scale_out, scale_in,
+    gathered_speeds, halo_out, halo_in, speed_out, speed_in, final_out, final_in, scale_out, scale_in,
     load_sem, facts_send, facts_recv, places_send, places_recv, first_send, first_recv,
     in_send, in_recv, part_send, part_recv, halo_send, halo_recv, speed_send, speed_recv,
     final_send, final_recv, scale_send, scale_recv,
@@ -761,32 +761,33 @@
     group = 32
 
     def tile(depth):
-        def blocks(index, carry):
-            source = index // (points // half)
-            lanes = pl.ds(pl.multiple_of(lax.rem(index, points // half) * half, half), half)
-            known = [targets[depth, k : k + 1, lanes] for k in range(3)]
-
+        known = [
+            [targets[depth, k : k + 1, lanes * half : (lanes + 1) * half] for k in range(3)]
+            for lanes in range(2)
+        ]
+
+        def blocks(source, carry):
             def rows_of(g, inner):
                 start = pl.multiple_of(g * group, group)
                 rows = pl.ds(start, group)
-                dx = known[0] - source_cols[source, 0, rows, :]
-                dy = known[1] - source_cols[source, 1, rows, :]
-                dz = known[2] - source_cols[source, 2, rows, :]
-                numerator = (
-                    source_cols[source, 3, rows, :] * dx
-                    + source_cols[source, 4, rows, :] * dy
-                    + source_cols[source, 5, rows, :] * dz
-                )
-                squared = dx * dx + dy * dy + dz * dz + SMOOTHING * SMOOTHING
-                inverse = lax.rsqrt(squared)
-                value = numerator * inverse * (inverse * inverse)
+                place_x, place_y, place_z, normal_x, normal_y, normal_z = [
+                    source_cols[source, k, rows, :] for k in range(6)
+                ]
                 deep = pl.ds(pl.multiple_of(source * points + start, group), group)
-                tiles[depth, deep, lanes] = value.astype(bf16)
+                for lanes in range(2):
+                    dx = known[lanes][0] - place_x
+                    dy = known[lanes][1] - place_y
+                    dz = known[lanes][2] - place_z
+                    numerator = normal_x * dx + normal_y * dy + normal_z * dz
+                    squared = dx * dx + dy * dy + dz * dz + SMOOTHING * SMOOTHING
+                    inverse = lax.rsqrt(squared)
+                    value = numerator * inverse * (inverse * inverse)
+                    tiles[depth, deep, tile_lanes(lanes)] = value.astype(bf16)
                 return inner
 
             return lax.fori_loop(0, points // group, rows_of, carry, unroll=2)
 
-        lax.fori_loop(0, members * (points // half), blocks, 0)
+        lax.fori_loop(0, members, blocks, 0)
 
     def send_pressures(repeat, speeds):
         @pl.loop(1, depth_count + 1)
@@ -803,8 +804,10 @@
                 @pl.when(d == 1)
                 def _():
                     each(1, members, lambda d: first_copy(d).wait_recv())
-
-            value = dot(speeds(), tiles[depth])
+                    for s in range(members):
+                        speeds[:, s * points : (s + 1) * points] = first_in[s]
+
+            value = dot(speeds[...], tiles[depth])
             if repeat == 0:
                 value = value + jnp.where(depth == z, 0.5, 0.0) * own_speed[...]
             part_out[repeat, depth] = value
@@ -852,9 +855,7 @@
                 if first <= c < first + REACH:
                     halo_out[step, part, side, c - first] = high
 
-    send_pressures(
-        0, lambda: jnp.concatenate([first_in[s] for s in range(members)], axis=1)
-    )
+    send_pressures(0, gathered_speeds)
 
     @pl.loop(0, members, unroll=2)
     def _(s):
@@ -918,7 +919,7 @@
                     for k in range(parts):
                         load[k, x * breadth + t * 4 + g] = value[own * k : own * (k + 1)]
 
-    def advance(part, step, final):
+    def advance(part, step, final, later_interior=False):
         now = lax.rem(step, 2)
         later = 1 - now
         for side, first in ((0, 0), (1, columns + REACH)):
@@ -968,16 +969,20 @@
         def _(pair):
             update(pair, pl.multiple_of(pair * 2 * block, 2 * block))
 
-        if not final:
+        if not final and not later_interior:
             interior(part, later)
 
     take_pressures(0)
 
-    @pl.loop(0, SUBSTEPS)
+    @pl.loop(0, SUBSTEPS - 1)
     def _(step):
         @pl.loop(0, parts)
         def _(part):
             advance(part, step, False)
+
+    @pl.loop(0, parts)
+    def _(part):
+        advance(part, SUBSTEPS - 1, False, True)
 
     for x in range(PAIR):
         for t in range(breadth // 4):
@@ -1010,15 +1015,20 @@
     ).astype(bf16)
     each(1, members, lambda d: speed_copy(d).start())
     speed_in[me] = speed_out[...]
+
+    @pl.loop(0, parts)
+    def _(part):
+        interior(part, SUBSTEPS % 2)
+
     each(1, members, lambda d: speed_copy(d).wait_recv())
 
-    def gathered():
-        arrived = [speed_in[s].astype(f32) for s in range(members)]
-        lower = jnp.concatenate([value[0:own] for value in arrived], axis=0)
-        upper = jnp.concatenate([value[own : 2 * own] for value in arrived], axis=0)
-        return jnp.concatenate([lower, upper], axis=1).astype(bf16)
-
-    send_pressures(1, gathered)
+    arrived = [speed_in[s].astype(f32) for s in range(members)]
+    for part in range(2):
+        pieces = [value[part * own : (part + 1) * own] for value in arrived]
+        gathered_speeds[:, part * pairs * points : (part + 1) * pairs * points] = (
+            jnp.concatenate(pieces, axis=0).astype(bf16)
+        )
+    send_pressures(1, gathered_speeds)
     take_pressures(1)
 
     @pl.loop(SUBSTEPS, last_step)
@@ -1153,6 +1163,7 @@
             VMEM((members, parts * own, count), f32),
             VMEM((columns, 8, half), f32),
             VMEM((LOADS, points), f32),
+            VMEM((LOADS, members * points), bf16),
             VMEM((steps, parts, 2, REACH, block, half), bf16),
             VMEM((steps, parts, 2, REACH, block, half), bf16),
             VMEM((2 * own, members // 2 * points), bf16),

time: 82.1 us -> 79.5 us (0.968)
  Pallas kernels: 77.4 us -> 74.8 us
    pallas_call x1, Pallas kernels: 77.4 us -> 74.8 us  [plane_on_device(): pl.pallas_call(functools.partial(plane_kernel, shape), out_shape=(state,...]
where the time goes in v4:
time: 79.5 us; the launch traced here: 79.3 us
  Pallas kernels  74.8 us (94%)
  local copies, waits for them, and re-layouts  3.81 us (5%)
    pallas_call x1, Pallas kernels, plane_on_device(): pl.pallas_call(functools.partial(plane_kernel, shape), out_shape=(state,...  74.8 us
    unnamed x12, local copies, waits for them, and re-layouts  3.81 us

profile of v4, /device:TPU:0, one launch (start us, length us, event | category | flops | bytes accessed | tf_op | source)
XLA Modules:
  0.0 79.3 jit_solution(17089845217277678292)
XLA Ops:
  0.6 0.0 copy-start.1
  0.6 0.0 copy-start
  0.7 0.0 copy-start.3
  0.7 0.7 copy-done.1
  1.3 0.0 copy-done
  1.3 0.0 copy-done.3
  1.3 0.0 copy-start.2
  1.3 0.7 copy-done.2
  2.0 0.0 copy-start.4
  2.0 0.7 copy-done.4
  2.7 74.8 %plane_steps.1 = (f32[3,512,128]{2,1,0:T(8,128)S(1)}, f32[3,512,128]{2,1,0:T(8,128)S(1)}) custom-call(f32[3,512,128]{2,1,0:T(8,128)} %bitcast.28, f32[3,512,128]{2,1,0:T(8,128)} %bitcast.29, f32[8,32]{1,0:T(8,128)S(1)} %bitcast.25, f32[3,256]{1,0:T(4,128)S(1)} %copy-done.1, f32[3,256]{1,0:T(4,128)S(1)} %copy-done.2, f32[1,256]{1,0:T(1,128)S(1)} %bitcast.26, ...), custom_call_target="tpu_custom_call" | custom-call | tf_op jit(solution)/shard_map/plane_steps/pallas_call | solution.py:1131
  77.6 0.9 %copy.11 = f32[3,32,8,256]{3,2,1,0:T(8,128)} copy(f32[3,32,8,256]{3,2,1,0:T(8,128)S(1)} %bitcast.24) | data formatting | bytes 1572864
  78.4 0.9 %copy.12 = f32[3,32,8,256]{3,2,1,0:T(8,128)} copy(f32[3,32,8,256]{3,2,1,0:T(8,128)S(1)} %bitcast.23) | data formatting | bytes 1572864
Async XLA Ops:
  0.6 0.7 copy-start.1
  0.6 0.7 copy-start
  0.7 0.7 copy-start.3
  1.3 0.7 copy-start.2
  2.0 0.7 copy-start.4

commit v5 on v4

--- a/solution.py
+++ b/solution.py
@@ -485,8 +485,8 @@
 
 def plane_kernel(
     shape, u_hbm, v_hbm, stiff_ref, position_ref, normal_ref, area_ref, map_ref, u_out, v_out,
-    u_raw, v_raw, perm, turn, eye, stencil, in_out, in_in, facts_out, facts, places, targets,
-    source_cols, first_out, first_in, tiles, part_out, part_in, spoken,
+    u_raw, v_raw, perm, eye, stencil, in_out, in_in, facts_out, facts, places, targets,
+    source_cols, first_out, first_in, tiles, part_out, part_in, far_out, far_in, spoken,
     onehot, onehot_back, u_now, v_now, load, halves, summed, patched, stiff_now, own_speed,
     gathered_speeds, halo_out, halo_in, speed_out, speed_in, final_out, final_in, scale_out, scale_in,
     load_sem, facts_send, facts_recv, places_send, places_recv, first_send, first_recv,
@@ -559,7 +559,6 @@
     square = (width, width)
     line, column = iota(square, 0), iota(square, 1)
     perm[0:width, :] = ones_where(lane_of(line) == column)
-    turn[...] = ones_where(lane_of(column) == line)
     outer = (LOADS, width)
     perm[width : width + LOADS, :] = ones_where(
         (layers - 1) * LOADS + iota(outer, 0) == iota(outer, 1)
@@ -618,10 +617,10 @@
     def speed_copy(d):
         return plane_copy(d, speed_out, speed_in, speed_send, speed_recv)
 
-    def final_copy(part, d):
+    def final_copy(part, f, d):
         return plane_copy(
-            d, final_out.at[part, member_of(d)], final_in.at[part],
-            final_send.at[part], final_recv.at[part],
+            d, final_out.at[part, f, member_of(d)], final_in.at[part, f],
+            final_send.at[part, f], final_recv.at[part, f],
         )
 
     def scale_copy(part, d):
@@ -629,14 +628,31 @@
             d, scale_out.at[part], scale_in.at[part], scale_send.at[part], scale_recv.at[part]
         )
 
-    def part_copy(repeat, dz, dj):
+    def side_of(depth):
+        return depth // (depth_count // 2)
+
+    def part_copy(repeat, dz, dj, far):
         lines = pl.ds(pl.multiple_of(member_of(dj) * own, own), own)
+        if far:
+            source, target = far_out.at[repeat, depth_of(dz), member_of(dj)], far_in
+        else:
+            source, target = part_out.at[repeat, depth_of(dz), lines, :], part_in
         return pltpu.make_async_remote_copy(
-            src_ref=part_out.at[repeat, depth_of(dz), lines, :],
-            dst_ref=part_in.at[repeat, z, me],
+            src_ref=source, dst_ref=target.at[repeat, z, me],
             send_sem=part_send.at[repeat, dz, dj], recv_sem=part_recv.at[repeat, dz, dj],
             device_id=device(depth_of(dz), member_of(dj)), device_id_type=MESH,
         )
+
+    def near_or_far(depth, action):
+        near = side_of(depth) == side_of(z)
+
+        @pl.when(near)
+        def _():
+            action(False)
+
+        @pl.when(jnp.logical_not(near))
+        def _():
+            action(True)
 
     def halo_copy(step, part, side, arriving):
         there = side if arriving else 1 - side
@@ -753,12 +769,12 @@
 
     each(1, members, lambda d: facts_copy(d).wait_recv())
 
-    @pl.loop(0, members)
+    @pl.loop(0, members, unroll=4)
     def _(s):
         for k in range(6):
             source_cols[s, k] = as_column(facts[s, k : k + 1, :])
 
-    group = 32
+    group = 64
 
     def tile(depth):
         known = [
@@ -810,26 +826,50 @@
             value = dot(speeds[...], tiles[depth])
             if repeat == 0:
                 value = value + jnp.where(depth == z, 0.5, 0.0) * own_speed[...]
-            part_out[repeat, depth] = value
-
-            @pl.when(d < depth_count)
-            def _():
-                each(0, members, lambda dj: part_copy(repeat, d, dj).start())
+            def pass_on(far):
+                if far:
+                    sides = [value[:, tile_lanes(t)].reshape(members, own, half) for t in range(2)]
+                    far_out[repeat, depth] = jnp.concatenate(sides, axis=1).astype(bf16)
+                else:
+                    part_out[repeat, depth] = value
+
+                @pl.when(d < depth_count)
+                def _():
+                    each(0, members, lambda dj: part_copy(repeat, d, dj, far).start())
+
+            near_or_far(depth, pass_on)
 
             @pl.when(d == depth_count)
             def _():
-                each(1, members, lambda dj: part_copy(repeat, 0, dj).start())
+                each(1, members, lambda dj: part_copy(repeat, 0, dj, False).start())
 
         part_in[repeat, z, me] = part_out[
             repeat, z, pl.ds(pl.multiple_of(me * own, own), own), :
         ]
 
-    def parts_taken(repeat, action):
-        each(1, members, lambda dj: action(part_copy(repeat, 0, dj)))
+    def parts_arrived(repeat):
+        each(1, members, lambda dj: part_copy(repeat, 0, dj, False).wait_recv())
 
         @pl.loop(1, depth_count)
         def _(d):
-            each(0, members, lambda dj: action(part_copy(repeat, d, dj)))
+            near_or_far(
+                lax.rem(z + depth_count - d, depth_count),
+                lambda far: each(
+                    0, members, lambda dj: part_copy(repeat, d, dj, far).wait_recv()
+                ),
+            )
+
+    def parts_sent(repeat):
+        each(1, members, lambda dj: part_copy(repeat, 0, dj, False).wait_send())
+
+        @pl.loop(1, depth_count)
+        def _(d):
+            near_or_far(
+                depth_of(d),
+                lambda far: each(
+                    0, members, lambda dj: part_copy(repeat, d, dj, far).wait_send()
+                ),
+            )
 
     def interior(part, now):
         lines = halves[now, part].reshape(columns // 2 * 2 * block, 2 * half)
@@ -892,13 +932,19 @@
         interior(part, 0)
 
     def take_pressures(repeat):
-        parts_taken(repeat, lambda copy: copy.wait_recv())
-
-        @pl.loop(0, members, unroll=4)
+        parts_arrived(repeat)
+        near_first = side_of(z) * (depth_count // 2)
+        far_first = depth_count // 2 - near_first
+
+        @pl.loop(0, members, unroll=8)
         def _(s):
-            value = part_in[repeat, 0, s]
-            for d in range(1, depth_count):
-                value = value + part_in[repeat, d, s]
+            value = part_in[repeat, near_first, s]
+            for d in range(1, depth_count // 2):
+                value = value + part_in[repeat, near_first + d, s]
+            rest = far_in[repeat, far_first, s].astype(f32)
+            for d in range(1, depth_count // 2):
+                rest = rest + far_in[repeat, far_first + d, s].astype(f32)
+            value = value + jnp.concatenate([rest[0:own], rest[own : 2 * own]], axis=1)
             if repeat > 0:
                 value = value + 0.5 * spoken[s]
             pieces = [
@@ -965,7 +1011,7 @@
         if not final:
             send_halos(step + 1, part)
 
-        @pl.loop(edge, columns // 2 - edge, unroll=2)
+        @pl.loop(edge, columns // 2 - edge, unroll=4)
         def _(pair):
             update(pair, pl.multiple_of(pair * 2 * block, 2 * block))
 
@@ -976,7 +1022,7 @@
 
     @pl.loop(0, SUBSTEPS - 1)
     def _(step):
-        @pl.loop(0, parts)
+        @pl.loop(0, parts, unroll=parts)
         def _(part):
             advance(part, step, False)
 
@@ -1033,7 +1079,7 @@
 
     @pl.loop(SUBSTEPS, last_step)
     def _(step):
-        @pl.loop(0, parts)
+        @pl.loop(0, parts, unroll=parts)
         def _(part):
             advance(part, step, False)
 
@@ -1041,36 +1087,42 @@
     def _(part):
         advance(part, last_step, True)
         done = 1 - last_step % 2
-        for f, state in enumerate((u_now.at[done, part, pl.ds(REACH, columns)], v_now.at[part])):
-            high = largest(state[...].reshape(columns * layers, own, half))
+        states = (u_now.at[done, part, pl.ds(REACH, columns)], v_now.at[part])
+        tops = [largest(state[...].reshape(columns * layers, own, half)) for state in states]
+        for f, top in enumerate(tops):
             scale_out[part, :, f * (half // 2) : (f + 1) * (half // 2)] = jnp.broadcast_to(
-                high * (1.0 / LEVELS), (1, half // 2)
+                top * (1.0 / LEVELS), (1, half // 2)
             )
-            inverse = LEVELS / high
+        each(1, members, lambda d: scale_copy(part, d).start())
+        for f, state in enumerate(states):
+            inverse = LEVELS / tops[f]
             for x in range(PAIR):
                 for t in range(breadth // 4):
                     given = [state[x * breadth + t * 4 + g] * inverse for g in range(4)]
                     for r, value in enumerate(exchange(given)):
-                        final_out[
-                            part, r * PAIR + x, f * block : (f + 1) * block, tile_lanes(t)
-                        ] = jnp.round(value).astype(i32).astype(i16)
-        each(1, members, lambda d: final_copy(part, d).start())
-        each(1, members, lambda d: scale_copy(part, d).start())
-        final_in[part, me] = final_out[part, me]
+                        final_out[part, f, r * PAIR + x, :, tile_lanes(t)] = (
+                            jnp.round(value).astype(i32).astype(i16)
+                        )
+            each(1, members, lambda d: final_copy(part, f, d).start())
+            final_in[part, f, me] = final_out[part, f, me]
         scale_in[part, me] = scale_out[part]
 
     @pl.loop(0, parts)
     def _(part):
-        each(1, members, lambda d: final_copy(part, d).wait_recv())
         each(1, members, lambda d: scale_copy(part, d).wait_recv())
-        value = final_in[part].astype(i32).astype(f32)
         for f, result in enumerate((u_out, v_out)):
+            each(1, members, lambda d: final_copy(part, f, d).wait_recv())
             scale = scale_in[part, :, :, f * (half // 2) : f * (half // 2) + 1]
-            rows = (value[:, f * block : (f + 1) * block] * scale).reshape(width, count)
+            rows = final_in[part, f].astype(i32).astype(f32) * scale
+            rows = jnp.concatenate(
+                [
+                    rows[:, layer * own : (layer + 1) * own].reshape(LOADS, count)
+                    for layer in range(layers)
+                ], axis=0
+            )
             high = rows.astype(bf16)
             low = (rows - high.astype(f32)).astype(bf16)
-            ordered = [dot(turn[...], piece).astype(bf16) for piece in (high, low)]
-            back = dot_turned(eye[...], ordered[0]) + dot_turned(eye[...], ordered[1])
+            back = dot_turned(eye[...], high) + dot_turned(eye[...], low)
             for j in range(breadth):
                 for lanes in range(2):
                     lines = pl.ds(lanes * breadth + j, height, stride=2 * breadth)
@@ -1084,11 +1136,12 @@
     each(1, members, lambda d: in_copy(d).wait_send())
     each(1, members, lambda d: speed_copy(d).wait_send())
     for repeat in range(COUPLED):
-        parts_taken(repeat, lambda copy: copy.wait_send())
+        parts_sent(repeat)
 
     @pl.loop(0, parts)
     def _(part):
-        each(1, members, lambda d: final_copy(part, d).wait_send())
+        for f in range(2):
+            each(1, members, lambda d: final_copy(part, f, d).wait_send())
         each(1, members, lambda d: scale_copy(part, d).wait_send())
 
         @pl.loop(0, last_step + 1)
@@ -1127,7 +1180,7 @@
     columns = PAIR * breadth
     anywhere = pl.BlockSpec(memory_space=pl.ANY)
     slab = (members, parts, 2 * block, count)
-    final = (parts, members, 2 * block, count)
+    final = (parts, 2, members, block, count)
     u_new, v_new = pl.pallas_call(
         functools.partial(plane_kernel, shape),
         out_shape=(state, state),
@@ -1137,7 +1190,6 @@
             VMEM(raw, f32),
             VMEM(raw, f32),
             VMEM((width + LOADS, width), bf16),
-            VMEM((width, width), bf16),
             VMEM((count, count), bf16),
             VMEM((count, count), bf16),
             VMEM(slab, i16),
@@ -1152,6 +1204,8 @@
             VMEM((depth_count, members * points, points), bf16),
             VMEM((COUPLED, depth_count, LOADS, points), f32),
             VMEM((COUPLED, depth_count, members, own, points), f32),
+            VMEM((COUPLED, depth_count, members, 2 * own, half), bf16),
+            VMEM((COUPLED, depth_count, members, 2 * own, half), bf16),
             VMEM((members, own, points), f32),
             VMEM((members, count, points), bf16),
             VMEM((members, points, count), bf16),
@@ -1187,8 +1241,8 @@
             dma((steps, parts, 2)),
             dma((members,)),
             dma((members,)),
-            dma((parts, members)),
-            dma((parts, members)),
+            dma((parts, 2, members)),
+            dma((parts, 2, members)),
             dma((parts, members)),
             dma((parts, members)),
         ],
@@ -1210,7 +1264,7 @@
     _, height, breadth, width = displacement.shape
     members = row_count * PAIR
     return (
-        col_count % PAIR == 0
+        col_count % (2 * PAIR) == 0
         and LOADS % members == 0
         and LOADS // members == 8
         and height * breadth == wet_map.shape[0] == width == 256

time: 79.5 us -> 77.1 us (0.970)
  Pallas kernels: 74.8 us -> 72.4 us
    pallas_call x1, Pallas kernels: 74.8 us -> 72.4 us  [plane_on_device(): pl.pallas_call(functools.partial(plane_kernel, shape), out_shape=(state,...]
where the time goes in v5:
time: 77.1 us; the launch traced here: 76.9 us
  Pallas kernels  72.4 us (94%)
  local copies, waits for them, and re-layouts  3.81 us (5%)
    pallas_call x1, Pallas kernels, plane_on_device(): pl.pallas_call(functools.partial(plane_kernel, shape), out_shape=(state,...  72.4 us
    unnamed x12, local copies, waits for them, and re-layouts  3.81 us

profile of v5, /device:TPU:0, one launch (start us, length us, event | category | flops | bytes accessed | tf_op | source)
XLA Modules:
  0.0 76.9 jit_solution(2351122141640012175)
XLA Ops:
  0.6 0.0 copy-start.1
  0.6 0.0 copy-start
  0.7 0.0 copy-start.3
  0.7 0.7 copy-done.1
  1.3 0.0 copy-done
  1.3 0.0 copy-done.3
  1.3 0.0 copy-start.2
  1.3 0.7 copy-done.2
  2.0 0.0 copy-start.4
  2.0 0.7 copy-done.4
  2.7 72.4 %plane_steps.1 = (f32[3,512,128]{2,1,0:T(8,128)S(1)}, f32[3,512,128]{2,1,0:T(8,128)S(1)}) custom-call(f32[3,512,128]{2,1,0:T(8,128)} %bitcast.28, f32[3,512,128]{2,1,0:T(8,128)} %bitcast.29, f32[8,32]{1,0:T(8,128)S(1)} %bitcast.25, f32[3,256]{1,0:T(4,128)S(1)} %copy-done.1, f32[3,256]{1,0:T(4,128)S(1)} %copy-done.2, f32[1,256]{1,0:T(1,128)S(1)} %bitcast.26, ...), custom_call_target="tpu_custom_call" | custom-call | tf_op jit(solution)/shard_map/plane_steps/pallas_call | solution.py:1184
  75.1 0.9 %copy.11 = f32[3,32,8,256]{3,2,1,0:T(8,128)} copy(f32[3,32,8,256]{3,2,1,0:T(8,128)S(1)} %bitcast.24) | data formatting | bytes 1572864
  76.0 0.9 %copy.12 = f32[3,32,8,256]{3,2,1,0:T(8,128)} copy(f32[3,32,8,256]{3,2,1,0:T(8,128)S(1)} %bitcast.23) | data formatting | bytes 1572864
Async XLA Ops:
  0.6 0.7 copy-start.1
  0.6 0.7 copy-start
  0.7 0.7 copy-start.3
  1.3 0.7 copy-start.2
  2.0 0.7 copy-start.4
